TPU v7x, 32 devices: a whole 2x2x4 slice. The times are simulated.
32 devices in a mesh: fsdp: 8 (over z, y), ctx: 4 (over x, core).
Axes of the slice: x: 2, y: 2, z: 4, core: 2. Of those that a mesh axis runs over, the one named last changes fastest.
Arguments:
- block_input: bfloat16 [8192, 1024], P(('fsdp', 'ctx')), may hold values from -6 to 6
- ln1_gain: bfloat16 [1024], P('fsdp'), may hold values from 0.5 to 1.5
- ln1_bias: bfloat16 [1024], P('fsdp'), may hold values from -1.5 to 1.5
- qkv_weight: bfloat16 [1024, 3, 1024], P('fsdp', None, 'ctx'), may hold values from -0.1875 to 0.1875
- qv_bias: bfloat16 [2, 1024], P(None, 'fsdp'), may hold values from -2.5 to 2.5
- out_weight: bfloat16 [1024, 1024], P(('ctx', 'fsdp')), may hold values from -1.5 to 1.5
- out_bias: bfloat16 [1024], P('fsdp'), may hold values from -1.5 to 1.5
- ln2_gain: bfloat16 [1024], P('fsdp'), may hold values from 0.5 to 1.5
- ln2_bias: bfloat16 [1024], P('fsdp'), may hold values from -1.5 to 1.5
- up_weight: bfloat16 [1024, 4096], P('fsdp', 'ctx'), may hold values from -0.1875 to 0.1875
- up_bias: bfloat16 [4096], P('fsdp'), may hold values from -2.5 to 2.5
- down_weight: bfloat16 [4096, 1024], P(('ctx', 'fsdp')), may hold values from -0.1875 to 0.1875
- down_bias: bfloat16 [1024], P('fsdp'), may hold values from -1.5 to 1.5
- doc_ids: int32 [8, 1024], P('fsdp'), may hold values from -1 to 7, as said below
- cotangent: bfloat16 [8192, 1024], P(('fsdp', 'ctx')), may hold values from -6 to 6
Outputs:
- output: bfloat16 [8192, 1024], P(('fsdp', 'ctx'))
- input_grad: float32 [8192, 1024], P(('fsdp', 'ctx'))
- ln1_gain_grad: float32 [1024], P('fsdp')
- ln1_bias_grad: float32 [1024], P('fsdp')
- qkv_weight_grad: float32 [1024, 3, 1024], P('fsdp', None, 'ctx')
- qv_bias_grad: float32 [2, 1024], P(None, 'fsdp')
- out_weight_grad: float32 [1024, 1024], P(('ctx', 'fsdp'))
- out_bias_grad: float32 [1024], P('fsdp')
- ln2_gain_grad: float32 [1024], P('fsdp')
- ln2_bias_grad: float32 [1024], P('fsdp')
- up_weight_grad: float32 [1024, 4096], P('fsdp', 'ctx')
- up_bias_grad: float32 [4096], P('fsdp')
- down_weight_grad: float32 [4096, 1024], P(('ctx', 'fsdp'))
- down_bias_grad: float32 [1024], P('fsdp')
Inputs may be any that keep to these rules, and one draw needn't show every extreme that they name: `doc_ids`: along each group, numbers start at 0 and rise by one from one sequence to the next; padding (-1) only at a group's end. A sequence holds 128 to 1024 positions, except that a group's last sequence may be cut short; some sequence holds exactly 1024; some group has no padding and some group is half padding.
All inputs are finite; a program needn't handle non-finite values.
Results may differ from a plain program's by a relative error of at most 0.02.
Values may be sent and summed in bfloat16 or wider, within the bound.
A program may use at most 128 MiB of HBM per device.

v0:
```python
import jax
import jax.numpy as jnp
from jax import lax
from jax.sharding import PartitionSpec as P

HD = 64
FF = 4096


eps = 1e-05


def normalize(values):
    centre = values - jnp.mean(values, axis=-1, keepdims=True)
    spread = jnp.mean(centre * centre, axis=-1, keepdims=True)
    return centre * lax.rsqrt(spread + eps)


def gelu_tanh(values):
    return (
        0.5
        * values
        * (1.0 + jnp.tanh(0.7978845608028654 * (values + 0.044715 * values * values * values)))
    )


def contract_rows(left, right):
    return lax.dot_general(
        left, right, (((0,), (0,)), ((), ())), preferred_element_type=jnp.float32
    )


def contract_cols(left, right):
    return lax.dot_general(
        left, right, (((1,), (1,)), ((), ())), preferred_element_type=jnp.float32
    )


def project(inputs, weight):
    return (
        jnp.dot(
            inputs,
            lax.all_gather(weight, "fsdp", axis=0, tiled=True),
            preferred_element_type=jnp.float32,
        ),
        weight,
    )


def project_back(grad_low, weight):
    return contract_cols(grad_low, lax.all_gather(weight, "fsdp", axis=0, tiled=True))


def gather_rows(values):
    return lax.all_gather(values, "ctx", axis=0, tiled=True)


def reduce_rows(partial_value):
    return lax.psum_scatter(
        partial_value.astype(jnp.bfloat16), "ctx", scatter_dimension=0, tiled=True
    ).astype(jnp.float32)


def weight_grad(inputs, grad_low):
    return lax.psum_scatter(
        contract_rows(inputs, grad_low).astype(jnp.bfloat16),
        "fsdp",
        scatter_dimension=0,
        tiled=True,
    ).astype(jnp.float32)


def block_scores(queries, keys_all, seq_ids, places, start, block, factor):
    query_blk = queries[start : start + block]
    scores = (
        jnp.einsum("qhd,khd->hqk", query_blk, keys_all, preferred_element_type=jnp.float32) * factor
    )
    allowed = (seq_ids[start : start + block, None] == seq_ids[None, :]) & (
        places[None, :] <= places[start : start + block, None]
    )
    return jnp.where(allowed[None], scores, -1000000000.0)


def attend(queries, keys_all, values_all, seq_ids, block, factor):
    places = jnp.arange(keys_all.shape[0], dtype=jnp.int32)
    outputs = []
    totals = []
    for start in range(0, keys_all.shape[0], block):
        scores = block_scores(queries, keys_all, seq_ids, places, start, block, factor)
        top = jnp.max(scores, axis=-1, keepdims=True)
        expo = jnp.exp(scores - top)
        summed = jnp.sum(expo, axis=-1, keepdims=True)
        probs_low = (expo / summed).astype(jnp.bfloat16)
        outputs.append(
            jnp.einsum("hqk,khd->qhd", probs_low, values_all, preferred_element_type=jnp.float32)
        )
        totals.append(top + jnp.log(summed))
    return (jnp.concatenate(outputs, 0), jnp.concatenate(totals, 1))


def attend_back(queries, keys_all, values_all, grad_heads, seq_ids, log_sums, block, factor):
    places = jnp.arange(keys_all.shape[0], dtype=jnp.int32)
    query_grads = []
    key_grad = jnp.zeros(keys_all.shape, jnp.float32)
    value_grad = jnp.zeros(values_all.shape, jnp.float32)
    for start in range(0, keys_all.shape[0], block):
        scores = block_scores(queries, keys_all, seq_ids, places, start, block, factor)
        probs = jnp.exp(scores - log_sums[:, start : start + block])
        grad_blk = grad_heads[start : start + block]
        grad_probs = jnp.einsum(
            "qhd,khd->hqk", grad_blk, values_all, preferred_element_type=jnp.float32
        )
        delta = jnp.sum(probs * grad_probs, axis=-1, keepdims=True)
        grad_scores = (probs * (grad_probs - delta)).astype(jnp.bfloat16)
        query_grads.append(
            jnp.einsum("hqk,khd->qhd", grad_scores, keys_all, preferred_element_type=jnp.float32)
            * factor
        )
        key_grad = (
            key_grad
            + jnp.einsum(
                "hqk,qhd->khd",
                grad_scores,
                queries[start : start + block],
                preferred_element_type=jnp.float32,
            )
            * factor
        )
        value_grad = value_grad + jnp.einsum(
            "hqk,qhd->khd", probs.astype(jnp.bfloat16), grad_blk, preferred_element_type=jnp.float32
        )
    return (jnp.concatenate(query_grads, 0), key_grad, value_grad)


def on_device(
    block_input,
    ln1_gain,
    ln1_bias,
    qkv_weight,
    qv_bias,
    out_weight,
    out_bias,
    ln2_gain,
    ln2_bias,
    up_weight,
    up_bias,
    down_weight,
    down_bias,
    doc_ids,
    cotangent,
):
    gain_one, shift_one, qv_full, out_shift, gain_two, shift_two, up_shift, down_shift = (
        lax.all_gather(ln1_gain, "fsdp", axis=0, tiled=True),
        lax.all_gather(ln1_bias, "fsdp", axis=0, tiled=True),
        lax.all_gather(qv_bias, "fsdp", axis=1, tiled=True),
        lax.all_gather(out_bias, "fsdp", axis=0, tiled=True),
        lax.all_gather(ln2_gain, "fsdp", axis=0, tiled=True),
        lax.all_gather(ln2_bias, "fsdp", axis=0, tiled=True),
        lax.all_gather(up_bias, "fsdp", axis=0, tiled=True),
        lax.all_gather(down_bias, "fsdp", axis=0, tiled=True),
    )
    rows = block_input.shape[0]
    model = block_input.shape[1]
    groups = lax.axis_size("ctx")
    place = lax.axis_index("ctx")
    capacity = rows * groups
    width = qkv_weight.shape[2]
    heads_here = width // HD
    hidden_here = up_weight.shape[1]
    factor = 1.0 / HD**0.5
    block = min(512, capacity)
    group_ids = doc_ids[0]
    own_ids = lax.dynamic_slice_in_dim(group_ids, place * rows, rows)
    qv_here = lax.dynamic_slice_in_dim(qv_full.astype(jnp.float32), place * width, width, 1)
    qkv_shift = jnp.concatenate([qv_here[0], jnp.zeros((width,), jnp.float32), qv_here[1]])
    up_here = lax.dynamic_slice_in_dim(
        up_shift.astype(jnp.float32), place * hidden_here, hidden_here, 0
    )
    qkv_flat = qkv_weight.reshape(qkv_weight.shape[0], 3 * width)
    input_float = block_input.astype(jnp.float32)
    norm_one = normalize(input_float)
    h_one = (norm_one * gain_one + shift_one).astype(jnp.bfloat16)
    h_one_all = gather_rows(h_one)
    qkv_proj, qkv_kept = project(h_one_all, qkv_flat)
    qkv = (qkv_proj + qkv_shift).astype(jnp.bfloat16).reshape(capacity, 3, heads_here, HD)
    queries = qkv[:, 0]
    keys_all = qkv[:, 1]
    values_all = qkv[:, 2]
    attended, log_sums = attend(queries, keys_all, values_all, group_ids, block, factor)
    mixed_all = attended.astype(jnp.bfloat16).reshape(capacity, width)
    out_part, out_kept = project(mixed_all, out_weight)
    resid = input_float + reduce_rows(out_part) + out_shift
    norm_two = normalize(resid)
    h_two = (norm_two * gain_two + shift_two).astype(jnp.bfloat16)
    h_two_all = gather_rows(h_two)
    up_proj, up_kept = project(h_two_all, up_weight)
    pre_act = up_proj + up_here
    act, gelu_back = jax.vjp(gelu_tanh, pre_act)
    act_low = act.astype(jnp.bfloat16)
    down_part, down_kept = project(act_low, down_weight)
    output = (resid + reduce_rows(down_part) + down_shift).astype(jnp.bfloat16)
    live = (own_ids >= 0).astype(jnp.float32)
    grad_out = cotangent.astype(jnp.float32) * live[:, None]
    grad_low = grad_out.astype(jnp.bfloat16)
    down_shift_grad = jnp.sum(grad_low.astype(jnp.float32), axis=0)
    grad_all = gather_rows(grad_low)
    down_grad = weight_grad(act_low, grad_all)
    grad_act = project_back(grad_all, down_weight)
    grad_pre = gelu_back(grad_act)[0].astype(jnp.bfloat16)
    up_grad = weight_grad(h_two_all, grad_pre)
    up_sums = jnp.sum(grad_pre.astype(jnp.float32), axis=0)
    up_shift_grad = lax.dynamic_update_slice_in_dim(
        jnp.zeros((FF,), jnp.float32), up_sums, place * hidden_here, 0
    )
    grad_h_two = reduce_rows(project_back(grad_pre, up_weight))
    gain_two_grad = jnp.sum(grad_h_two * norm_two, axis=0)
    shift_two_grad = jnp.sum(grad_h_two, axis=0)
    unused_two, norm_back_two = jax.vjp(normalize, resid)
    grad_resid = grad_out + norm_back_two(grad_h_two * gain_two.astype(jnp.float32))[0]
    resid_low = grad_resid.astype(jnp.bfloat16)
    out_shift_grad = jnp.sum(resid_low.astype(jnp.float32), axis=0)
    resid_all = gather_rows(resid_low)
    out_grad = weight_grad(mixed_all, resid_all)
    grad_heads = (
        project_back(resid_all, out_weight).astype(jnp.bfloat16).reshape(capacity, heads_here, HD)
    )
    query_grad, key_grad, value_grad = attend_back(
        queries, keys_all, values_all, grad_heads, group_ids, log_sums, block, factor
    )
    grad_qkv = (
        jnp.stack([query_grad, key_grad, value_grad], 1)
        .astype(jnp.bfloat16)
        .reshape(capacity, 3 * width)
    )
    qkv_grad = weight_grad(h_one_all, grad_qkv).reshape(qkv_weight.shape[0], 3, width)
    column_sums = jnp.sum(grad_qkv.astype(jnp.float32), axis=0).reshape(3, width)
    qv_local = jnp.stack([column_sums[0], column_sums[2]])
    qv_grad = lax.dynamic_update_slice_in_dim(
        jnp.zeros((2, model), jnp.float32), qv_local, place * width, 1
    )
    grad_h_one = reduce_rows(project_back(grad_qkv, qkv_flat))
    gain_one_grad = jnp.sum(grad_h_one * norm_one, axis=0)
    shift_one_grad = jnp.sum(grad_h_one, axis=0)
    unused_one, norm_back_one = jax.vjp(normalize, input_float)
    input_grad = grad_resid + norm_back_one(grad_h_one * gain_one.astype(jnp.float32))[0]
    (
        gain_one_part,
        shift_one_part,
        qv_part,
        out_shift_part,
        gain_two_part,
        shift_two_part,
        up_shift_part,
        down_shift_part,
    ) = (
        lax.psum_scatter(
            gain_one_grad.astype(jnp.bfloat16), "fsdp", scatter_dimension=0, tiled=True
        ).astype(jnp.float32),
        lax.psum_scatter(
            shift_one_grad.astype(jnp.bfloat16), "fsdp", scatter_dimension=0, tiled=True
        ).astype(jnp.float32),
        lax.psum_scatter(
            qv_grad.astype(jnp.bfloat16), "fsdp", scatter_dimension=1, tiled=True
        ).astype(jnp.float32),
        lax.psum_scatter(
            out_shift_grad.astype(jnp.bfloat16), "fsdp", scatter_dimension=0, tiled=True
        ).astype(jnp.float32),
        lax.psum_scatter(
            gain_two_grad.astype(jnp.bfloat16), "fsdp", scatter_dimension=0, tiled=True
        ).astype(jnp.float32),
        lax.psum_scatter(
            shift_two_grad.astype(jnp.bfloat16), "fsdp", scatter_dimension=0, tiled=True
        ).astype(jnp.float32),
        lax.psum_scatter(
            up_shift_grad.astype(jnp.bfloat16), "fsdp", scatter_dimension=0, tiled=True
        ).astype(jnp.float32),
        lax.psum_scatter(
            down_shift_grad.astype(jnp.bfloat16), "fsdp", scatter_dimension=0, tiled=True
        ).astype(jnp.float32),
    )
    (
        gain_one_sum,
        shift_one_sum,
        qv_sum,
        out_shift_sum,
        gain_two_sum,
        shift_two_sum,
        up_shift_sum,
        down_shift_sum,
    ) = lax.psum(
        (
            gain_one_part,
            shift_one_part,
            qv_part,
            out_shift_part,
            gain_two_part,
            shift_two_part,
            up_shift_part,
            down_shift_part,
        ),
        "ctx",
    )
    return (
        output,
        input_grad,
        gain_one_sum,
        shift_one_sum,
        qkv_grad,
        qv_sum,
        out_grad,
        out_shift_sum,
        gain_two_sum,
        shift_two_sum,
        up_grad,
        up_shift_sum,
        down_grad,
        down_shift_sum,
    )


def solution(mesh):
    placed = (
        P(("fsdp", "ctx"), None),
        P("fsdp"),
        P("fsdp"),
        P("fsdp", None, "ctx"),
        P(None, "fsdp"),
        P(("ctx", "fsdp"), None),
        P("fsdp"),
        P("fsdp"),
        P("fsdp"),
        P("fsdp", "ctx"),
        P("fsdp"),
        P(("ctx", "fsdp"), None),
        P("fsdp"),
        P("fsdp", None),
        P(("fsdp", "ctx"), None),
    )
    return jax.shard_map(
        on_device,
        mesh=mesh,
        in_specs=placed,
        out_specs=(
            P(("fsdp", "ctx"), None),
            P(("fsdp", "ctx"), None),
            P("fsdp"),
            P("fsdp"),
            P("fsdp", None, "ctx"),
            P(None, "fsdp"),
            P(("ctx", "fsdp"), None),
            P("fsdp"),
            P("fsdp"),
            P("fsdp"),
            P("fsdp", "ctx"),
            P("fsdp"),
            P(("ctx", "fsdp"), None),
            P("fsdp"),
        ),
        check_vma=False,
    )
```

profile of v0, /device:TPU:8, one launch (start us, length us, event | category | flops | bytes accessed | tf_op | source)
XLA Modules:
  0.0 836.1 jit_solution(12191915348453404416)
XLA Ops:
  9.0 18.1 %all-gather = bf16[8,1,128]{2,1,0:T(2,128)(2,1)S(1)} all-gather(bf16[1,1,128]{2,1,0:T(2,128)(2,1)} %bitcast.160), channel_id=1, replica_groups=mesh['fsdp'=8,'ctx'=4] {'fsdp'}, dimensions={0}, use_global_device_ids=true | all-gather | bytes 2304 | tf_op jit(solution)/shard_map/all_gather | solution.py:153
  27.1 16.4 %all-gather.1 = bf16[8,1,128]{2,1,0:T(2,128)(2,1)S(1)} all-gather(bf16[1,1,128]{2,1,0:T(2,128)(2,1)} %bitcast.161), channel_id=1, replica_groups=mesh['fsdp'=8,'ctx'=4] {'fsdp'}, dimensions={0}, use_global_device_ids=true | all-gather | bytes 2304 | tf_op jit(solution)/shard_map/all_gather | solution.py:154
  48.3 18.3 %all_gather.56 = bf16[2,1024]{1,0:T(2,128)(2,1)S(1)} all-gather(bf16[2,128]{1,0:T(2,128)(2,1)} %param.19), channel_id=1, replica_groups=mesh['fsdp'=8,'ctx'=4] {'fsdp'}, dimensions={1}, use_global_device_ids=true | all-gather | bytes 4608 | tf_op jit(solution)/shard_map/all_gather | solution.py:155
  67.3 31.8 %all_gather.57 = bf16[256,1024]{1,0:T(8,128)(2,1)S(1)} all-gather(bf16[32,1024]{1,0:T(8,128)(2,1)} %param.20), channel_id=1, replica_groups=mesh['fsdp'=8,'ctx'=4] {'fsdp'}, dimensions={0}, use_global_device_ids=true | all-gather | bytes 589824 | tf_op jit(solution)/shard_map/all_gather | solution.py:43
  122.1 16.1 %all-gather.2 = bf16[8,1,128]{2,1,0:T(2,128)(2,1)S(1)} all-gather(bf16[1,1,128]{2,1,0:T(2,128)(2,1)S(1)} %bitcast.162), channel_id=1, replica_groups=mesh['fsdp'=8,'ctx'=4] {'fsdp'}, dimensions={0}, use_global_device_ids=true | all-gather | bytes 2304 | tf_op jit(solution)/shard_map/all_gather | solution.py:156
  138.2 18.0 %all-gather.3 = bf16[8,1,128]{2,1,0:T(2,128)(2,1)S(1)} all-gather(bf16[1,1,128]{2,1,0:T(2,128)(2,1)S(1)} %bitcast.163), channel_id=1, replica_groups=mesh['fsdp'=8,'ctx'=4] {'fsdp'}, dimensions={0}, use_global_device_ids=true | all-gather | bytes 2304 | tf_op jit(solution)/shard_map/all_gather | solution.py:157
  156.3 16.5 %all-gather.4 = bf16[8,1,128]{2,1,0:T(2,128)(2,1)S(1)} all-gather(bf16[1,1,128]{2,1,0:T(2,128)(2,1)S(1)} %bitcast.164), channel_id=1, replica_groups=mesh['fsdp'=8,'ctx'=4] {'fsdp'}, dimensions={0}, use_global_device_ids=true | all-gather | bytes 2304 | tf_op jit(solution)/shard_map/all_gather | solution.py:158
  180.3 27.9 %all-gather.5 = bf16[8,1,512]{2,1,0:T(2,128)(2,1)S(1)} all-gather(bf16[1,1,512]{2,1,0:T(2,128)(2,1)S(1)} %reshape.269), channel_id=1, replica_groups=mesh['fsdp'=8,'ctx'=4] {'fsdp'}, dimensions={0}, use_global_device_ids=true | all-gather | bytes 9216 | tf_op jit(solution)/shard_map/all_gather | solution.py:159
  208.3 19.4 %all-gather.19.cloned.1.call-done = bf16[1024,1024]{1,0:T(8,128)(2,1)} async-done(((bf16[256,1024]{1,0:T(8,128)(2,1)}), bf16[1024,1024]{1,0:T(8,128)(2,1)}) %all-gather.19.cloned.1.call-update) | async-done | bytes 2097168 | tf_op jit(solution)/shard_map/all_gather | solution.py:55
  234.2 18.2 %all-gather.25.cloned.1.call-done = bf16[1024,1024]{1,0:T(8,128)(2,1)} async-done(((bf16[256,1024]{1,0:T(8,128)(2,1)}), bf16[1024,1024]{1,0:T(8,128)(2,1)}) %all-gather.25.cloned.1.call-update) | async-done | bytes 2097168 | tf_op jit(solution)/shard_map/all_gather | solution.py:55
  252.4 51.7 %all-gather.23.cloned.1.call-done = bf16[1024,1024]{1,0:T(8,128)(2,1)} async-done(((bf16[128,1024]{1,0:T(8,128)(2,1)}), bf16[1024,1024]{1,0:T(8,128)(2,1)}) %all-gather.23.cloned.1.call-update) | async-done | bytes 2097168 | tf_op jit(solution)/shard_map/all_gather | solution.py:43
  304.1 9.0 %convert_reduce_fusion = (bf16[1024]{0:T(1024)(128)(2,1)S(1)}, bf16[1024,1024]{1,0:T(8,128)(2,1)S(1)}) fusion(f32[1024,1024]{1,0:T(8,128)} %fusion.72, f32[1024]{0:T(1024)S(1)} %dynamic_slice.10, bf16[1024,1024]{1,0:T(8,128)(2,1)} %all-gather.25.cloned.1.call-done, bf16[1024,1024]{1,0:T(8,128)(2,1)} %all-gather.23.cloned.1.call-done), kind=kOutput, calls=%fused_computation.28 | convolution fusion | flops 2175794176 | bytes 10491904 | tf_op jit(solution)/shard_map/dot_general | solution.py:34
  325.8 15.2 %all-gather.6 = bf16[8,1,128]{2,1,0:T(2,128)(2,1)S(1)} all-gather(bf16[1,1,128]{2,1,0:T(2,128)(2,1)S(1)} %bitcast.165), channel_id=1, replica_groups=mesh['fsdp'=8,'ctx'=4] {'fsdp'}, dimensions={0}, use_global_device_ids=true | all-gather | bytes 2304 | tf_op jit(solution)/shard_map/all_gather | solution.py:160
  341.0 7.2 reduce-scatter.16.cloned.1.call-done
  349.8 32.4 %reduce-scatter.14.cloned.1.call-done = bf16[256,1024]{1,0:T(8,128)(2,1)} async-done(((bf16[1024,1024]{1,0:T(8,128)(2,1)}), bf16[256,1024]{1,0:T(8,128)(2,1)}) %reduce-scatter.14.cloned.1.call-update) | async-done | bytes 524304 | tf_op jit(solution)/shard_map/reduce_scatter | solution.py:59
  392.9 7.8 convolution_convert_fusion
  401.0 8.6 %all-gather.27.cloned.1.call-done = bf16[1024,1024]{1,0:T(8,128)(2,1)} async-done(((bf16[256,1024]{1,0:T(8,128)(2,1)}), bf16[1024,1024]{1,0:T(8,128)(2,1)}) %all-gather.27.cloned.1.call-update) | async-done | bytes 2097168 | tf_op jit(solution)/shard_map/all_gather | solution.py:55
  456.8 23.9 %reduce-scatter.24.cloned.1.call-done = bf16[128,1024]{1,0:T(8,128)(2,1)} async-done(((bf16[1024,1024]{1,0:T(8,128)(2,1)}), bf16[128,1024]{1,0:T(8,128)(2,1)}) %reduce-scatter.24.cloned.1.call-update) | async-done | bytes 262160 | tf_op jit(solution)/shard_map/reduce_scatter | solution.py:65
  482.6 68.9 %reduce-scatter.26.cloned.1.call-done = bf16[128,1024]{1,0:T(8,128)(2,1)} async-done(((bf16[1024,1024]{1,0:T(8,128)(2,1)}), bf16[128,1024]{1,0:T(8,128)(2,1)}) %reduce-scatter.26.cloned.1.call-update) | async-done | bytes 262160 | tf_op jit(solution)/shard_map/reduce_scatter | solution.py:65
  553.2 63.3 %reduce-scatter.28.cloned.1.call-done = bf16[128,2]{1,0:T(8,128)(2,1)} async-done(((bf16[1024,2]{1,0:T(8,128)(2,1)}), bf16[128,2]{1,0:T(8,128)(2,1)}) %reduce-scatter.28.cloned.1.call-update) | async-done | bytes 528
  617.3 63.8 %reduce-scatter.22.cloned.1.call-done = bf16[32,1024]{1,0:T(8,128)(2,1)} async-done(((bf16[256,1024]{1,0:T(8,128)(2,1)}), bf16[32,1024]{1,0:T(8,128)(2,1)}) %reduce-scatter.22.cloned.1.call-update) | async-done | bytes 65552 | tf_op jit(solution)/shard_map/reduce_scatter | solution.py:65
  682.6 65.3 %reduce-scatter.20.cloned.1.call-done = bf16[128,768]{1,0:T(8,128)(2,1)} async-done(((bf16[1024,768]{1,0:T(8,128)(2,1)}), bf16[128,768]{1,0:T(8,128)(2,1)}) %reduce-scatter.20.cloned.1.call-update) | async-done | bytes 196624 | tf_op jit(solution)/shard_map/reduce_scatter | solution.py:65
  749.9 31.3 %reduce-scatter.18.cloned.1.call-done = bf16[256,1024]{1,0:T(8,128)(2,1)} async-done(((bf16[1024,1024]{1,0:T(8,128)(2,1)}), bf16[256,1024]{1,0:T(8,128)(2,1)}) %reduce-scatter.18.cloned.1.call-update) | async-done | bytes 524304 | tf_op jit(solution)/shard_map/reduce_scatter | solution.py:59
  785.5 34.4 %all-reduce.8 = (bf16[1024]{0:T(1024)(128)(2,1)S(1)}, bf16[1024]{0:T(1024)(128)(2,1)S(1)}, bf16[1024]{0:T(1024)(128)(2,1)S(1)}, bf16[1024]{0:T(1024)(128)(2,1)S(...) all-reduce(bf16[1024]{0:T(1024)(128)(2,1)S(1)} %get-tuple-element.5, ...), channel_id=6, replica_groups=mesh['fsdp'=8,'ctx'=4] {'fsdp'}, use_global_device_ids=true, to_apply=%region_19.20.clone | all-reduce | flops 10240 | bytes 40960
  (193 shorter events, 136.4 us)
Async XLA Ops:
  7.2 93.8 %all-gather.17.cloned.1.call-start = ((), (), s32[]{:S(2)}) async-start(), calls=%async_computation.10 | async-start | bytes 1769472 | tf_op jit(solution)/shard_map/all_gather | solution.py:43
  9.0 92.0 %all-gather.15.cloned.1.call-start = ((), (), s32[]{:S(2)}) async-start(), calls=%async_computation.9 | async-start | bytes 2621440 | tf_op jit(solution)/shard_map/all_gather | solution.py:55
  48.2 124.7 %reduce-scatter.12.cloned.1.call-start = ((), (), s32[]{:S(2)}) async-start(), calls=%async_computation.11 | async-start | bytes 2621440 | tf_op jit(solution)/shard_map/reduce_scatter | solution.py:59
  119.3 58.4 %copy-start.16 = (bf16[4,64,512]{2,1,0:T(8,128)(2,1)}, bf16[4,64,512]{2,1,0:T(8,128)(2,1)S(1)}, u32[]{:S(2)}) copy-start(bf16[4,64,512]{2,1,0:T(8,128)(2,1)S(1)} %fusion.38) | copy-start | bytes 786436
  119.3 18.9 %copy-start.20 = (bf16[128]{0:T(256)(128)(2,1)S(1)}, bf16[128]{0:T(256)(128)(2,1)}, u32[]{:S(2)}) copy-start(bf16[128]{0:T(256)(128)(2,1)} %param.22) | copy-start | bytes 772
  119.3 37.0 %copy-start.21 = (bf16[128]{0:T(256)(128)(2,1)S(1)}, bf16[128]{0:T(256)(128)(2,1)}, u32[]{:S(2)}) copy-start(bf16[128]{0:T(256)(128)(2,1)} %param.23) | copy-start | bytes 772
  119.3 53.5 %copy-start.2 = (bf16[256,1024]{1,0:T(8,128)(2,1)S(1)}, bf16[256,1024]{1,0:T(8,128)(2,1)}, u32[]{:S(2)}) copy-start(bf16[256,1024]{1,0:T(8,128)(2,1)} %param.15) | copy-start | bytes 1572868
  119.4 59.1 %copy-start.8 = (bf16[256,1024]{1,0:T(8,128)(2,1)S(1)}, bf16[256,1024]{1,0:T(8,128)(2,1)}, u32[]{:S(2)}) copy-start(bf16[256,1024]{1,0:T(8,128)(2,1)} %param.29) | copy-start | bytes 1572868
  121.4 58.8 %copy-start.18 = (bf16[512]{0:T(512)(128)(2,1)S(1)}, bf16[512]{0:T(512)(128)(2,1)}, u32[]{:S(2)}) copy-start(bf16[512]{0:T(512)(128)(2,1)} %param.25) | copy-start | bytes 3076
  121.5 86.8 %all-gather.21.cloned.1.call-start = ((), (), s32[]{:S(2)}) async-start(), calls=%async_computation.13 | async-start | bytes 2359296 | tf_op jit(solution)/shard_map/all_gather | solution.py:43
  122.0 105.7 %all-gather.19.cloned.1.call-start = ((), (), s32[]{:S(2)}) async-start(), calls=%async_computation.12 | async-start | bytes 2621440 | tf_op jit(solution)/shard_map/all_gather | solution.py:55
  177.7 74.7 %all-gather.25.cloned.1.call-start = ((), (), s32[]{:S(2)}) async-start(), calls=%async_computation.16 | async-start | bytes 2621440 | tf_op jit(solution)/shard_map/all_gather | solution.py:55
  179.5 124.6 %all-gather.23.cloned.1.call-start = ((), (), s32[]{:S(2)}) async-start(), calls=%async_computation.14 | async-start | bytes 2359296 | tf_op jit(solution)/shard_map/all_gather | solution.py:43
  180.2 168.0 %reduce-scatter.16.cloned.1.call-start = ((), (), s32[]{:S(2)}) async-start(), calls=%async_computation.17 | async-start | bytes 2621440 | tf_op jit(solution)/shard_map/reduce_scatter | solution.py:59
  318.2 30.0 %copy-start.3 = (bf16[256,1024]{1,0:T(8,128)(2,1)S(1)}, bf16[256,1024]{1,0:T(8,128)(2,1)}, u32[]{:S(2)}) copy-start(bf16[256,1024]{1,0:T(8,128)(2,1)} %reduce-scatter.12.cloned.1.call-done) | copy-start | bytes 1572868
  318.2 64.0 %reduce-scatter.14.cloned.1.call-start = ((), (), s32[]{:S(2)}) async-start(), calls=%async_computation.15 | async-start | bytes 2621440 | tf_op jit(solution)/shard_map/reduce_scatter | solution.py:59
  325.7 83.8 %all-gather.27.cloned.1.call-start = ((), (), s32[]{:S(2)}) async-start(), calls=%async_computation.18 | async-start | bytes 2621440 | tf_op jit(solution)/shard_map/all_gather | solution.py:55
  386.8 93.9 %reduce-scatter.24.cloned.1.call-start = ((), (), s32[]{:S(2)}) async-start(), calls=%async_computation.22 | async-start | bytes 2359296 | tf_op jit(solution)/shard_map/reduce_scatter | solution.py:65
  392.9 158.6 %reduce-scatter.26.cloned.1.call-start = ((), (), s32[]{:S(2)}) async-start(), calls=%async_computation.23 | async-start | bytes 2359296 | tf_op jit(solution)/shard_map/reduce_scatter | solution.py:65
  400.8 215.7 %reduce-scatter.28.cloned.1.call-start = ((), (), s32[]{:S(2)}) async-start(), calls=%async_computation.24 | async-start | bytes 294912
  441.1 240.0 %reduce-scatter.22.cloned.1.call-start = ((), (), s32[]{:S(2)}) async-start(), calls=%async_computation.21 | async-start | bytes 589824 | tf_op jit(solution)/shard_map/reduce_scatter | solution.py:65
  444.4 303.5 %reduce-scatter.20.cloned.1.call-start = ((), (), s32[]{:S(2)}) async-start(), calls=%async_computation.20 | async-start | bytes 1769472 | tf_op jit(solution)/shard_map/reduce_scatter | solution.py:65
  449.4 331.9 %reduce-scatter.18.cloned.1.call-start = ((), (), s32[]{:S(2)}) async-start(), calls=%async_computation.19 | async-start | bytes 2621440 | tf_op jit(solution)/shard_map/reduce_scatter | solution.py:59
  454.5 372.3 %copy-start.5 = (f32[256,1024]{1,0:T(8,128)S(1)}, f32[256,1024]{1,0:T(8,128)}, u32[]{:S(2)}) copy-start(f32[256,1024]{1,0:T(8,128)} %copy-done.4) | copy-start | bytes 3145732
  (22 other events, 106.5 us)
Sparse Core Ops, SparseCore 0:
  10.6 45.0 all-gather.16
  57.8 22.2 all-gather.14
  121.6 31.2 reduce-scatter.11
  155.1 49.4 all-gather.20
  206.6 21.0 all-gather.18
  229.8 22.5 all-gather.24
  254.8 49.2 all-gather.22
  318.3 29.8 reduce-scatter.15
  350.8 31.4 reduce-scatter.13
  387.0 22.5 all-gather.26
  413.5 67.1 reduce-scatter.23
  484.6 66.8 reduce-scatter.25
  555.7 60.7 reduce-scatter.27
  620.0 61.0 reduce-scatter.21
  684.4 63.5 reduce-scatter.19
  750.5 30.7 reduce-scatter.17
where the time goes:
time: 849 us; the launch traced here: 836 us
  waiting for transfers between devices  456 us (54%)
  blocking collectives  219 us (26%)
  matrix products  87.6 us (10%)
  other arithmetic  41.8 us (5%)
  between operations  16.1 us (2%)
  local copies, waits for them, and re-layouts  14.1 us (2%)
    reduce_scatter x4, waiting for transfers between devices, weight_grad(): lax.psum_scatter(contract_rows(inputs, grad_low).astype(jnp.bfloat16), 'f...  222 us
    reduce_scatter x4, waiting for transfers between devices, reduce_rows(): lax.psum_scatter(partial_value.astype(jnp.bfloat16), 'ctx', scatter_dimen...  70.9 us
    unnamed x17, waiting for transfers between devices  64.7 us
    all_gather x3, waiting for transfers between devices, project(): lax.all_gather(weight, 'fsdp', axis=0, tiled=True)  51.7 us
    all_gather x4, waiting for transfers between devices, gather_rows(): return lax.all_gather(values, 'ctx', axis=0, tiled=True)  46.2 us
    unnamed x1, blocking collectives  34.4 us
    all_gather x1, blocking collectives, project(): lax.all_gather(weight, 'fsdp', axis=0, tiled=True)  31.8 us
    all_gather x1, blocking collectives, on_device(): lax.all_gather(up_bias, 'fsdp', axis=0, tiled=True)  27.9 us
  transfers between devices with their start and end apart: 16, of which 12 were waited for; matrix products, arithmetic and copies ran while one was open for 11% of the time, Pallas kernels for 0%

commit v1 on v0

--- a/solution.py
+++ b/solution.py
@@ -36,38 +36,126 @@
     )
 
 
+def split_fsdp():
+    total = lax.axis_size("fsdp")
+    inner = 2 if total <= 8 else 8
+    return total // inner, inner
+
+
+def move_fsdp(values, outer_step, inner_step):
+    outer, inner = split_fsdp()
+    pairs = [
+        (a * inner + b, (a + outer_step) % outer * inner + (b + inner_step) % inner)
+        for a in range(outer)
+        for b in range(inner)
+    ]
+    return lax.ppermute(values, "fsdp", pairs)
+
+
+def move_ctx(values, chip_step, core_step):
+    chips = lax.axis_size("ctx") // 2
+    pairs = [
+        (x * 2 + c, (x + chip_step) % chips * 2 + (c + core_step) % 2)
+        for x in range(chips)
+        for c in range(2)
+    ]
+    return lax.ppermute(values, "ctx", pairs)
+
+
+def put(buffer, values, place, axis):
+    return lax.dynamic_update_index_in_dim(buffer, values, place, axis)
+
+
+def pick(buffer, place, axis):
+    return lax.dynamic_index_in_dim(buffer, place, axis, keepdims=False)
+
+
+def gather_weight(shard):
+    outer, inner = split_fsdp()
+    place = lax.axis_index("fsdp")
+    a, b = place // inner, place % inner
+    held = put(jnp.zeros((outer,) + shard.shape, shard.dtype), shard, a, 0)
+    for step in range(1, outer):
+        held = put(held, move_fsdp(shard, step, 0), (a + outer - step) % outer, 0)
+    if inner == 2:
+        other = move_fsdp(held, 0, 1)
+        first = b == 0
+        whole = jnp.stack([jnp.where(first, held, other), jnp.where(first, other, held)], 1)
+    else:
+        whole = put(jnp.zeros((outer, inner) + shard.shape, shard.dtype), held, b, 1)
+        for step in range(1, inner):
+            whole = put(whole, move_fsdp(held, 0, step), (b + inner - step) % inner, 1)
+    return whole.reshape((outer * inner,) + shard.shape)
+
+
+def scatter_fsdp(parts, sent_type):
+    outer, inner = split_fsdp()
+    place = lax.axis_index("fsdp")
+    a, b = place // inner, place % inner
+    parts = parts.reshape((outer, inner) + parts.shape[1:])
+    held = pick(parts, b, 1).astype(jnp.float32)
+    for step in range(1, inner):
+        sent = pick(parts, (b + step) % inner, 1).astype(sent_type)
+        held = held + move_fsdp(sent, 0, step).astype(jnp.float32)
+    summed = pick(held, a, 0)
+    for step in range(1, outer):
+        sent = pick(held, (a + step) % outer, 0).astype(sent_type)
+        summed = summed + move_fsdp(sent, step, 0).astype(jnp.float32)
+    return summed
+
+
+def gather_rows(values):
+    groups = lax.axis_size("ctx")
+    chips = groups // 2
+    place = lax.axis_index("ctx")
+    x, core = place // 2, place % 2
+    whole = jnp.zeros((groups,) + values.shape, values.dtype)
+    for step in range(chips):
+        got = values if step == 0 else move_ctx(values, step, 0)
+        origin = (x + chips - step) % chips * 2
+        whole = put(whole, got, origin + core, 0)
+        whole = put(whole, move_ctx(got, 0, 1), origin + 1 - core, 0)
+    return whole.reshape((groups * values.shape[0],) + values.shape[1:])
+
+
+def reduce_rows(parts):
+    groups = lax.axis_size("ctx")
+    chips = groups // 2
+    place = lax.axis_index("ctx")
+    x, core = place // 2, place % 2
+    parts = parts.reshape((chips, 2, parts.shape[0] // groups) + parts.shape[1:])
+    sent = pick(parts, 1 - core, 1).astype(jnp.bfloat16)
+    held = pick(parts, core, 1) + move_ctx(sent, 0, 1).astype(jnp.float32)
+    summed = pick(held, x, 0)
+    for step in range(1, chips):
+        sent = pick(held, (x + step) % chips, 0).astype(jnp.bfloat16)
+        summed = summed + move_ctx(sent, step, 0).astype(jnp.float32)
+    return summed
+
+
+def sum_ctx(values):
+    chips = lax.axis_size("ctx") // 2
+    total = values + move_ctx(values, 0, 1)
+    whole = total
+    for step in range(1, chips):
+        whole = whole + move_ctx(total, step, 0)
+    return whole
+
+
 def project(inputs, weight):
-    return (
-        jnp.dot(
-            inputs,
-            lax.all_gather(weight, "fsdp", axis=0, tiled=True),
-            preferred_element_type=jnp.float32,
-        ),
-        weight,
-    )
+    return jnp.dot(inputs, weight, preferred_element_type=jnp.float32)
 
 
 def project_back(grad_low, weight):
-    return contract_cols(grad_low, lax.all_gather(weight, "fsdp", axis=0, tiled=True))
-
-
-def gather_rows(values):
-    return lax.all_gather(values, "ctx", axis=0, tiled=True)
-
-
-def reduce_rows(partial_value):
-    return lax.psum_scatter(
-        partial_value.astype(jnp.bfloat16), "ctx", scatter_dimension=0, tiled=True
-    ).astype(jnp.float32)
+    return contract_cols(grad_low, weight)
 
 
 def weight_grad(inputs, grad_low):
-    return lax.psum_scatter(
-        contract_rows(inputs, grad_low).astype(jnp.bfloat16),
-        "fsdp",
-        scatter_dimension=0,
-        tiled=True,
-    ).astype(jnp.float32)
+    shards = lax.axis_size("fsdp")
+    full = contract_rows(inputs, grad_low)
+    return scatter_fsdp(
+        full.reshape(shards, full.shape[0] // shards, full.shape[1]), jnp.bfloat16
+    )
 
 
 def block_scores(queries, keys_all, seq_ids, places, start, block, factor):
@@ -149,15 +237,19 @@
     doc_ids,
     cotangent,
 ):
-    gain_one, shift_one, qv_full, out_shift, gain_two, shift_two, up_shift, down_shift = (
-        lax.all_gather(ln1_gain, "fsdp", axis=0, tiled=True),
-        lax.all_gather(ln1_bias, "fsdp", axis=0, tiled=True),
-        lax.all_gather(qv_bias, "fsdp", axis=1, tiled=True),
-        lax.all_gather(out_bias, "fsdp", axis=0, tiled=True),
-        lax.all_gather(ln2_gain, "fsdp", axis=0, tiled=True),
-        lax.all_gather(ln2_bias, "fsdp", axis=0, tiled=True),
-        lax.all_gather(up_bias, "fsdp", axis=0, tiled=True),
-        lax.all_gather(down_bias, "fsdp", axis=0, tiled=True),
+    shards = lax.axis_size("fsdp")
+    small = jnp.concatenate(
+        [
+            ln1_gain,
+            ln1_bias,
+            qv_bias[0],
+            qv_bias[1],
+            out_bias,
+            ln2_gain,
+            ln2_bias,
+            down_bias,
+            up_bias,
+        ]
     )
     rows = block_input.shape[0]
     model = block_input.shape[1]
@@ -171,48 +263,63 @@
     block = min(512, capacity)
     group_ids = doc_ids[0]
     own_ids = lax.dynamic_slice_in_dim(group_ids, place * rows, rows)
+    input_all = gather_rows(block_input)
+    small_all = gather_weight(small.reshape(-1, 128)).reshape(shards, small.shape[0])
+    piece = model // shards
+    gain_one, shift_one, query_shift, value_shift, out_shift, gain_two, shift_two, down_shift = (
+        small_all[:, i * piece : (i + 1) * piece].reshape(model) for i in range(8)
+    )
+    up_shift = small_all[:, 8 * piece :].reshape(-1)
+    qv_full = jnp.stack([query_shift, value_shift])
+    qkv_flat = gather_weight(qkv_weight.reshape(qkv_weight.shape[0], 3 * width)).reshape(
+        model, 3 * width
+    )
+    out_full = gather_weight(out_weight).reshape(width, model)
+    up_full = gather_weight(up_weight).reshape(model, hidden_here)
+    down_full = gather_weight(down_weight).reshape(hidden_here, model)
+    cot_all = gather_rows(cotangent)
     qv_here = lax.dynamic_slice_in_dim(qv_full.astype(jnp.float32), place * width, width, 1)
     qkv_shift = jnp.concatenate([qv_here[0], jnp.zeros((width,), jnp.float32), qv_here[1]])
     up_here = lax.dynamic_slice_in_dim(
         up_shift.astype(jnp.float32), place * hidden_here, hidden_here, 0
     )
-    qkv_flat = qkv_weight.reshape(qkv_weight.shape[0], 3 * width)
     input_float = block_input.astype(jnp.float32)
     norm_one = normalize(input_float)
-    h_one = (norm_one * gain_one + shift_one).astype(jnp.bfloat16)
-    h_one_all = gather_rows(h_one)
-    qkv_proj, qkv_kept = project(h_one_all, qkv_flat)
+    h_one_all = (normalize(input_all.astype(jnp.float32)) * gain_one + shift_one).astype(
+        jnp.bfloat16
+    )
+    qkv_proj = project(h_one_all, qkv_flat)
     qkv = (qkv_proj + qkv_shift).astype(jnp.bfloat16).reshape(capacity, 3, heads_here, HD)
     queries = qkv[:, 0]
     keys_all = qkv[:, 1]
     values_all = qkv[:, 2]
     attended, log_sums = attend(queries, keys_all, values_all, group_ids, block, factor)
     mixed_all = attended.astype(jnp.bfloat16).reshape(capacity, width)
-    out_part, out_kept = project(mixed_all, out_weight)
+    out_part = project(mixed_all, out_full)
     resid = input_float + reduce_rows(out_part) + out_shift
     norm_two = normalize(resid)
     h_two = (norm_two * gain_two + shift_two).astype(jnp.bfloat16)
     h_two_all = gather_rows(h_two)
-    up_proj, up_kept = project(h_two_all, up_weight)
+    up_proj = project(h_two_all, up_full)
     pre_act = up_proj + up_here
     act, gelu_back = jax.vjp(gelu_tanh, pre_act)
     act_low = act.astype(jnp.bfloat16)
-    down_part, down_kept = project(act_low, down_weight)
+    down_part = project(act_low, down_full)
     output = (resid + reduce_rows(down_part) + down_shift).astype(jnp.bfloat16)
     live = (own_ids >= 0).astype(jnp.float32)
     grad_out = cotangent.astype(jnp.float32) * live[:, None]
     grad_low = grad_out.astype(jnp.bfloat16)
     down_shift_grad = jnp.sum(grad_low.astype(jnp.float32), axis=0)
-    grad_all = gather_rows(grad_low)
+    grad_all = jnp.where(group_ids[:, None] >= 0, cot_all, jnp.zeros_like(cot_all))
     down_grad = weight_grad(act_low, grad_all)
-    grad_act = project_back(grad_all, down_weight)
+    grad_act = project_back(grad_all, down_full)
     grad_pre = gelu_back(grad_act)[0].astype(jnp.bfloat16)
     up_grad = weight_grad(h_two_all, grad_pre)
     up_sums = jnp.sum(grad_pre.astype(jnp.float32), axis=0)
     up_shift_grad = lax.dynamic_update_slice_in_dim(
         jnp.zeros((FF,), jnp.float32), up_sums, place * hidden_here, 0
     )
-    grad_h_two = reduce_rows(project_back(grad_pre, up_weight))
+    grad_h_two = reduce_rows(project_back(grad_pre, up_full))
     gain_two_grad = jnp.sum(grad_h_two * norm_two, axis=0)
     shift_two_grad = jnp.sum(grad_h_two, axis=0)
     unused_two, norm_back_two = jax.vjp(normalize, resid)
@@ -222,7 +329,7 @@
     resid_all = gather_rows(resid_low)
     out_grad = weight_grad(mixed_all, resid_all)
     grad_heads = (
-        project_back(resid_all, out_weight).astype(jnp.bfloat16).reshape(capacity, heads_here, HD)
+        project_back(resid_all, out_full).astype(jnp.bfloat16).reshape(capacity, heads_here, HD)
     )
     query_grad, key_grad, value_grad = attend_back(
         queries, keys_all, values_all, grad_heads, group_ids, log_sums, block, factor
@@ -243,63 +350,36 @@
     shift_one_grad = jnp.sum(grad_h_one, axis=0)
     unused_one, norm_back_one = jax.vjp(normalize, input_float)
     input_grad = grad_resid + norm_back_one(grad_h_one * gain_one.astype(jnp.float32))[0]
-    (
-        gain_one_part,
-        shift_one_part,
-        qv_part,
-        out_shift_part,
-        gain_two_part,
-        shift_two_part,
-        up_shift_part,
-        down_shift_part,
-    ) = (
-        lax.psum_scatter(
-            gain_one_grad.astype(jnp.bfloat16), "fsdp", scatter_dimension=0, tiled=True
-        ).astype(jnp.float32),
-        lax.psum_scatter(
-            shift_one_grad.astype(jnp.bfloat16), "fsdp", scatter_dimension=0, tiled=True
-        ).astype(jnp.float32),
-        lax.psum_scatter(
-            qv_grad.astype(jnp.bfloat16), "fsdp", scatter_dimension=1, tiled=True
-        ).astype(jnp.float32),
-        lax.psum_scatter(
-            out_shift_grad.astype(jnp.bfloat16), "fsdp", scatter_dimension=0, tiled=True
-        ).astype(jnp.float32),
-        lax.psum_scatter(
-            gain_two_grad.astype(jnp.bfloat16), "fsdp", scatter_dimension=0, tiled=True
-        ).astype(jnp.float32),
-        lax.psum_scatter(
-            shift_two_grad.astype(jnp.bfloat16), "fsdp", scatter_dimension=0, tiled=True
-        ).astype(jnp.float32),
-        lax.psum_scatter(
-            up_shift_grad.astype(jnp.bfloat16), "fsdp", scatter_dimension=0, tiled=True
-        ).astype(jnp.float32),
-        lax.psum_scatter(
-            down_shift_grad.astype(jnp.bfloat16), "fsdp", scatter_dimension=0, tiled=True
-        ).astype(jnp.float32),
-    )
+    packed = jnp.concatenate(
+        [
+            part.reshape(shards, -1)
+            for part in (
+                gain_one_grad,
+                shift_one_grad,
+                qv_grad[0],
+                qv_grad[1],
+                out_shift_grad,
+                gain_two_grad,
+                shift_two_grad,
+                down_shift_grad,
+                up_shift_grad,
+            )
+        ],
+        1,
+    )
+    sums = sum_ctx(scatter_fsdp(packed.reshape(shards, -1, 128), jnp.float32)).reshape(-1)
     (
         gain_one_sum,
         shift_one_sum,
-        qv_sum,
+        query_sum,
+        value_sum,
         out_shift_sum,
         gain_two_sum,
         shift_two_sum,
-        up_shift_sum,
         down_shift_sum,
-    ) = lax.psum(
-        (
-            gain_one_part,
-            shift_one_part,
-            qv_part,
-            out_shift_part,
-            gain_two_part,
-            shift_two_part,
-            up_shift_part,
-            down_shift_part,
-        ),
-        "ctx",
-    )
+    ) = (sums[i * piece : (i + 1) * piece] for i in range(8))
+    qv_sum = jnp.stack([query_sum, value_sum])
+    up_shift_sum = sums[8 * piece :]
     return (
         output,
         input_grad,

time: 849 us -> 429 us (0.51)
  waiting for transfers between devices: 456 us -> 116 us
  blocking collectives: 219 us -> 0 us
  local copies, waits for them, and re-layouts: 14.1 us -> 109 us
  starting transfers between devices: 1.51 us -> 73.5 us
  matrix products: 87.6 us -> 73.2 us
  between operations: 16.1 us -> 2.3 us
    reduce_scatter x8 -> x0, waiting for transfers between devices: 293 us -> none  [the longest x4 222 us: weight_grad(): lax.psum_scatter(contract_rows(inputs, grad_low).astype(jnp.bfloat16), 'f...]
    all_gather x9 -> x0, blocking collectives: 178 us -> none  [the longest x1 31.8 us: project(): lax.all_gather(weight, 'fsdp', axis=0, tiled=True)]
    ppermute x0 -> x62, waiting for transfers between devices: none -> 116 us  [the longest x40 74.3 us: move_fsdp(): return lax.ppermute(values, 'fsdp', pairs)]
    all_gather x7 -> x0, waiting for transfers between devices: 97.9 us -> none  [the longest x3 51.7 us: project(): lax.all_gather(weight, 'fsdp', axis=0, tiled=True)]
    ppermute x0 -> x62, starting transfers between devices: none -> 73.5 us  [the longest x40 64.4 us: move_fsdp(): return lax.ppermute(values, 'fsdp', pairs)]
    unnamed x17 -> x0, waiting for transfers between devices: 64.7 us -> none
    unnamed x1 -> x0, blocking collectives: 34.4 us -> none
    dynamic_update_slice x0 -> x34, local copies, waits for them, and re-layouts: none -> 22.3 us  [put(): return lax.dynamic_update_index_in_dim(buffer, values, place, axis)]
  transfers between devices with their start and end apart: 16 -> 62, of which waited for: 12 -> 24; matrix products, arithmetic and copies ran while one was open for 11% -> 36% of each run, Pallas kernels for 0% -> 0%
where the time goes in v1:
time: 429 us; the launch traced here: 423 us
  waiting for transfers between devices  116 us (27%)
  local copies, waits for them, and re-layouts  109 us (25%)
  starting transfers between devices  73.5 us (17%)
  matrix products  73.2 us (17%)
  other arithmetic  48.6 us (11%)
    ppermute x40, waiting for transfers between devices, move_fsdp(): return lax.ppermute(values, 'fsdp', pairs)  74.3 us
    ppermute x40, starting transfers between devices, move_fsdp(): return lax.ppermute(values, 'fsdp', pairs)  64.4 us
    ppermute x22, waiting for transfers between devices, move_ctx(): return lax.ppermute(values, 'ctx', pairs)  41.7 us
    unnamed x128, local copies, waits for them, and re-layouts  30.8 us
    dynamic_update_slice x34, local copies, waits for them, and re-layouts, put(): return lax.dynamic_update_index_in_dim(buffer, values, place, axis)  22.3 us
    dot_general x4, matrix products, contract_cols(): lax.dot_general(left, right, (((1,), (1,)), ((), ())), preferred_element_...  19.3 us
    dot_general x4, matrix products, project(): return jnp.dot(inputs, weight, preferred_element_type=jnp.float32)  16.3 us
    dot_general x4, matrix products, contract_rows(): lax.dot_general(left, right, (((0,), (0,)), ((), ())), preferred_element_...  9.46 us
  transfers between devices with their start and end apart: 62, of which 24 were waited for; matrix products, arithmetic and copies ran while one was open for 36% of the time, Pallas kernels for 0%

profile of v1, /device:TPU:8, one launch (start us, length us, event | category | flops | bytes accessed | tf_op | source)
XLA Modules:
  0.0 422.7 jit_solution(7953515138907192990)
XLA Ops:
  44.1 5.3 %collective-permute-start.12 = (bf16[32,1024]{1,0:T(8,128)(2,1)S(1)}, bf16[32,1024]{1,0:T(8,128)(2,1)S(1)}, u32[]{:S(2)}, u32[]{:S(2)}) collective-permute-start(bf16[32,1024]{1,0:T(8,128)(2,1)S(1)} %copy-done.43), channel_id=1, source_target_pairs={{0,16},{4,20},{8,24},{12,28},{16,0},{20,4},{24,8},{28,12},{1,17},{... | collective-permute-start | bytes 196616 | tf_op jit(solution)/shard_map/ppermute | solution.py:52
  56.0 3.9 collective-permute-start.1
  76.8 10.2 %collective-permute-done.21 = bf16[128,1024]{1,0:T(8,128)(2,1)} collective-permute-done((bf16[128,1024]{1,0:T(8,128)(2,1)}, bf16[128,1024]{1,0:T(8,128)(2,1)}, u32[]{:S(2)}, u32[]{:S(2)}) %collective-permute-start.21) | collective-permute-done | bytes 262176 | tf_op jit(solution)/shard_map/ppermute | solution.py:52
  91.5 4.0 collective-permute-done.14
  105.4 10.0 %collective-permute-done.10 = bf16[4,128,768]{2,1,0:T(8,128)(2,1)S(1)} collective-permute-done((bf16[4,128,768]{2,1,0:T(8,128)(2,1)}, bf16[4,128,768]{2,1,0:T(8,128)(2,1)S(1)}, u32[]{:S(2)}, u32[]{:S(2)}) %collective-permute-start.10) | collective-permute-done | bytes 786464 | tf_op jit(solution)/shard_map/ppermute | solution.py:52
  162.7 11.4 %collective-permute-done.16 = bf16[256,1024]{1,0:T(8,128)(2,1)S(1)} collective-permute-done((bf16[256,1024]{1,0:T(8,128)(2,1)S(1)}, bf16[256,1024]{1,0:T(8,128)(2,1)S(1)}, u32[]{:S(2)}, u32[]{:S(2)}) %collective-permute-start.16) | collective-permute-done | bytes 524320 | tf_op jit(solution)/shard_map/ppermute | solution.py:62
  181.4 9.4 %collective-permute-done.18 = bf16[256,1024]{1,0:T(8,128)(2,1)S(1)} collective-permute-done((bf16[256,1024]{1,0:T(8,128)(2,1)S(1)}, bf16[256,1024]{1,0:T(8,128)(2,1)S(1)}, u32[]{:S(2)}, u32[]{:S(2)}) %collective-permute-start.18) | collective-permute-done | bytes 524320 | tf_op jit(solution)/shard_map/ppermute | solution.py:62
  196.6 4.1 copy.85
  200.7 8.0 %fusion.14 = (bf16[1024,1024]{0,1:T(8,128)(2,1)}, f32[1024,1024]{1,0:T(8,128)}) fusion(f32[1024]{0:T(1024)S(1)} %dynamic_slice.162, bf16[1024,1024]{1,0:T(8,128)(2,1)} %bitcast.62, bf16[1024,1024]{1,0:T(8,128)(2,1)} %bitcast.519), kind=kOutput, calls=%fused_computation.31 | convolution fusion | flops 2157969408 | bytes 10489856 | tf_op jit(solution)/shard_map/dot_general | solution.py:146
  208.7 4.0 copy.102
  212.7 4.5 %fusion.135 = f32[4,2,128,1024]{3,2,1,0:T(8,128)S(1)} fusion(bf16[4,2,128,1024]{3,2,1,0:T(8,128)(2,1)} %bitcast.526, bf16[1024,1024,1,1]{1,0,3,2:T(8,128)(2,1)} %bitcast.512), kind=kOutput, calls=%fused_computation.326 | convolution fusion | flops 2147483648 | bytes 8388608 | tf_op jit(solution)/shard_map/dot_general | solution.py:28
  221.9 5.3 %copy.66 = f32[1024,1024]{0,1:T(8,128)} copy(f32[1024,1024]{1,0:T(8,128)} %get-tuple-element.133) | data formatting | bytes 8388608 | tf_op jit(solution)/shard_map/add | solution.py:304
  227.2 9.9 %convert_reduce_fusion = (f32[1024]{0:T(1024)S(1)}, bf16[1024,1024]{0,1:T(8,128)(2,1)}, bf16[1024,1024]{0,1:T(8,128)(2,1)}) fusion(f32[1024,1024]{0,1:T(8,128)} %copy.66, bf16[1024,1024]{1,0:T(8,128)(2,1)} %bitcast.513, bf16[1024,1024]{1,0:T(8,128)(2,1)} %bitcast.521), kind=kOutput, calls=%fused_computation.36 | convolution fusion | flops 2176842752 | bytes 12587008 | tf_op jit(solution)/shard_map/dot_general | solution.py:34
  237.2 3.9 copy.98
  241.1 4.5 %fusion.131 = f32[2,2,256,1024]{3,2,1,0:T(8,128)S(1)} fusion(bf16[2,2,256,1024]{3,2,1,0:T(8,128)(2,1)} %bitcast.525, bf16[1024,1024,1,1]{1,0,3,2:T(8,128)(2,1)} %bitcast.522), kind=kOutput, calls=%fused_computation.322 | convolution fusion | flops 2147483648 | bytes 8388608 | tf_op jit(solution)/shard_map/dot_general | solution.py:146
  248.2 4.3 %copy.99 = bf16[1024,1024]{1,0:T(8,128)(2,1)} copy(bf16[1024,1024]{0,1:T(8,128)(2,1)} %get-tuple-element.49) | data formatting | bytes 4194304 | tf_op jit(solution)/shard_map/dot_general | solution.py:34
  252.5 4.7 %fusion.132 = f32[2,2,256,1024]{3,2,1,0:T(8,128)S(1)} fusion(bf16[2,2,256,1024]{3,2,1,0:T(8,128)(2,1)} %bitcast.527, bf16[1024,1024,1,1]{1,0,3,2:T(8,128)(2,1)} %bitcast.520), kind=kOutput, calls=%fused_computation.323 | convolution fusion | flops 2147483648 | bytes 8388608 | tf_op jit(solution)/shard_map/dot_general | solution.py:34
  273.2 13.7 %collective-permute-done.54 = bf16[4,128,1024]{2,1,0:T(8,128)(2,1)S(1)} collective-permute-done((bf16[4,128,1024]{2,1,0:T(8,128)(2,1)S(1)}, bf16[4,128,1024]{2,1,0:T(8,128)(2,1)S(1)}, u32[]{:S(2)}, u32[]{:S(2)}) %collective-permute-start.54) | collective-permute-done | bytes 1048608 | tf_op jit(solution)/shard_map/ppermute | solution.py:52
  291.4 8.8 %collective-permute-done.29 = bf16[256,1024]{1,0:T(8,128)(2,1)S(1)} collective-permute-done((bf16[256,1024]{1,0:T(8,128)(2,1)S(1)}, bf16[256,1024]{1,0:T(8,128)(2,1)S(1)}, u32[]{:S(2)}, u32[]{:S(2)}) %collective-permute-start.29) | collective-permute-done | bytes 524320 | tf_op jit(solution)/shard_map/ppermute | solution.py:62
  310.9 8.0 %collective-permute-done.56 = bf16[128,1024]{1,0:T(8,128)(2,1)} collective-permute-done((bf16[128,1024]{1,0:T(8,128)(2,1)}, bf16[128,1024]{1,0:T(8,128)(2,1)}, u32[]{:S(2)}, u32[]{:S(2)}) %collective-permute-start.56) | collective-permute-done | bytes 262176 | tf_op jit(solution)/shard_map/ppermute | solution.py:52
  331.7 3.8 fusion.50
  353.4 3.8 fusion.27
  373.6 10.2 %collective-permute-done.39 = bf16[256,1024]{1,0:T(8,128)(2,1)S(1)} collective-permute-done((bf16[256,1024]{1,0:T(8,128)(2,1)S(1)}, bf16[256,1024]{1,0:T(8,128)(2,1)S(1)}, u32[]{:S(2)}, u32[]{:S(2)}) %collective-permute-start.39) | collective-permute-done | bytes 524320 | tf_op jit(solution)/shard_map/ppermute | solution.py:62
  411.1 4.8 %collective-permute-done.47 = bf16[128,768]{1,0:T(8,128)(2,1)S(1)} collective-permute-done((bf16[128,768]{1,0:T(8,128)(2,1)S(1)}, bf16[128,768]{1,0:T(8,128)(2,1)S(1)}, u32[]{:S(2)}, u32[]{:S(2)}) %collective-permute-start.47) | collective-permute-done | bytes 196640 | tf_op jit(solution)/shard_map/ppermute | solution.py:52
  (425 shorter events, 259.7 us)
Async XLA Ops:
  2.4 57.5 %collective-permute-start.7 = (bf16[128,768]{0,1:T(8,128)(2,1)}, bf16[128,768]{0,1:T(8,128)(2,1)}, u32[]{:S(2)}, u32[]{:S(2)}) collective-permute-start(bf16[128,768]{0,1:T(8,128)(2,1)} %bitcast.18), channel_id=1, source_target_pairs={{0,8},{4,12},{8,16},{12,20},{16,24},{20,28},{24,0},{28,4},{1,9},{5... | collective-permute-start | bytes 589832 | tf_op jit(solution)/shard_map/ppermute | solution.py:52
  4.0 59.9 %collective-permute-start.8 = (bf16[128,768]{0,1:T(8,128)(2,1)}, bf16[128,768]{0,1:T(8,128)(2,1)}, u32[]{:S(2)}, u32[]{:S(2)}) collective-permute-start(bf16[128,768]{0,1:T(8,128)(2,1)} %bitcast.18), channel_id=1, source_target_pairs={{0,16},{4,20},{8,24},{12,28},{16,0},{20,4},{24,8},{28,12},{1,17},{... | collective-permute-start | bytes 589832 | tf_op jit(solution)/shard_map/ppermute | solution.py:52
  5.0 60.7 %collective-permute-start.9 = (bf16[128,768]{0,1:T(8,128)(2,1)}, bf16[128,768]{0,1:T(8,128)(2,1)}, u32[]{:S(2)}, u32[]{:S(2)}) collective-permute-start(bf16[128,768]{0,1:T(8,128)(2,1)} %bitcast.18), channel_id=1, source_target_pairs={{0,24},{4,28},{8,0},{12,4},{16,8},{20,12},{24,16},{28,20},{1,25},{... | collective-permute-start | bytes 589832 | tf_op jit(solution)/shard_map/ppermute | solution.py:52
  7.0 89.3 %collective-permute-start = (bf16[256,1024]{1,0:T(8,128)(2,1)}, bf16[256,1024]{1,0:T(8,128)(2,1)}, u32[]{:S(2)}, u32[]{:S(2)}) collective-permute-start(bf16[256,1024]{1,0:T(8,128)(2,1)} %param.15), channel_id=1, source_target_pairs={{0,1},{1,0},{2,3},{3,2},{4,5},{5,4},{6,7},{7,6},{8,9},{9,8},{10,11... | collective-permute-start | bytes 1572872 | tf_op jit(solution)/shard_map/ppermute | solution.py:62
  56.0 43.2 %collective-permute-start.1 = (bf16[256,1024]{1,0:T(8,128)(2,1)S(1)}, bf16[256,1024]{1,0:T(8,128)(2,1)}, u32[]{:S(2)}, u32[]{:S(2)}) collective-permute-start(bf16[256,1024]{1,0:T(8,128)(2,1)S(1)} %copy-done.3), channel_id=1, source_target_pairs={{0,2},{1,3},{2,0},{3,1},{4,6},{5,7},{6,4},{7,5},{8,10},{9,11},{10,... | collective-permute-start | bytes 1572872 | tf_op jit(solution)/shard_map/ppermute | solution.py:62
  63.9 39.8 %collective-permute-start.30 = (bf16[256,1024]{1,0:T(8,128)(2,1)S(1)}, bf16[256,1024]{1,0:T(8,128)(2,1)}, u32[]{:S(2)}, u32[]{:S(2)}) collective-permute-start(bf16[256,1024]{1,0:T(8,128)(2,1)S(1)} %copy-done.16), channel_id=1, source_target_pairs={{0,1},{1,0},{2,3},{3,2},{4,5},{5,4},{6,7},{7,6},{8,9},{9,8},{10,11... | collective-permute-start | bytes 1572872 | tf_op jit(solution)/shard_map/ppermute | solution.py:62
  65.6 21.4 %collective-permute-start.21 = (bf16[128,1024]{1,0:T(8,128)(2,1)}, bf16[128,1024]{1,0:T(8,128)(2,1)}, u32[]{:S(2)}, u32[]{:S(2)}) collective-permute-start(bf16[128,1024]{1,0:T(8,128)(2,1)} %param.24), channel_id=1, source_target_pairs={{0,16},{4,20},{8,24},{12,28},{16,0},{20,4},{24,8},{28,12},{1,17},{... | collective-permute-start | bytes 786440 | tf_op jit(solution)/shard_map/ppermute | solution.py:52
  95.4 51.9 %collective-permute-start.24 = (bf16[128,1024]{1,0:T(8,128)(2,1)}, bf16[128,1024]{1,0:T(8,128)(2,1)}, u32[]{:S(2)}, u32[]{:S(2)}) collective-permute-start(bf16[128,1024]{1,0:T(8,128)(2,1)} %param.26), channel_id=1, source_target_pairs={{0,8},{4,12},{8,16},{12,20},{16,24},{20,28},{24,0},{28,4},{1,9},{5... | collective-permute-start | bytes 786440 | tf_op jit(solution)/shard_map/ppermute | solution.py:52
  96.3 19.1 %collective-permute-start.10 = (bf16[4,128,768]{2,1,0:T(8,128)(2,1)}, bf16[4,128,768]{2,1,0:T(8,128)(2,1)S(1)}, u32[]{:S(2)}, u32[]{:S(2)}) collective-permute-start(bf16[4,128,768]{2,1,0:T(8,128)(2,1)} %constant_dynamic-update-slice_fusion.1), channel_id=1, source_target_pairs={{0,4},{4,0},{8,12},{12,8},{16,20},{20,16},{24,28},{28,24},{1,5},{5... | collective-permute-start | bytes 2359304 | tf_op jit(solution)/shard_map/ppermute | solution.py:52
  99.2 49.8 %collective-permute-start.25 = (bf16[128,1024]{1,0:T(8,128)(2,1)}, bf16[128,1024]{1,0:T(8,128)(2,1)S(1)}, u32[]{:S(2)}, u32[]{:S(2)}) collective-permute-start(bf16[128,1024]{1,0:T(8,128)(2,1)} %param.26), channel_id=1, source_target_pairs={{0,16},{4,20},{8,24},{12,28},{16,0},{20,4},{24,8},{28,12},{1,17},{... | collective-permute-start | bytes 786440 | tf_op jit(solution)/shard_map/ppermute | solution.py:52
  115.4 34.3 %collective-permute-start.26 = (bf16[128,1024]{1,0:T(8,128)(2,1)}, bf16[128,1024]{1,0:T(8,128)(2,1)}, u32[]{:S(2)}, u32[]{:S(2)}) collective-permute-start(bf16[128,1024]{1,0:T(8,128)(2,1)} %param.26), channel_id=1, source_target_pairs={{0,24},{4,28},{8,0},{12,4},{16,8},{20,12},{24,16},{28,20},{1,25},{... | collective-permute-start | bytes 786440 | tf_op jit(solution)/shard_map/ppermute | solution.py:52
  119.1 58.7 %collective-permute-start.23 = (bf16[4,128,1024]{2,1,0:T(8,128)(2,1)}, bf16[4,128,1024]{2,1,0:T(8,128)(2,1)}, u32[]{:S(2)}, u32[]{:S(2)}) collective-permute-start(bf16[4,128,1024]{2,1,0:T(8,128)(2,1)} %bitcast_dynamic-update-slice_fusion.20), channel_id=1, source_target_pairs={{0,4},{4,0},{8,12},{12,8},{16,20},{20,16},{24,28},{28,24},{1,5},{5... | collective-permute-start | bytes 3145736 | tf_op jit(solution)/shard_map/ppermute | solution.py:52
  151.4 28.3 %collective-permute-start.27 = (bf16[4,128,1024]{2,1,0:T(8,128)(2,1)}, bf16[4,128,1024]{2,1,0:T(8,128)(2,1)}, u32[]{:S(2)}, u32[]{:S(2)}) collective-permute-start(bf16[4,128,1024]{2,1,0:T(8,128)(2,1)} %bitcast_dynamic-update-slice_fusion.16), channel_id=1, source_target_pairs={{0,4},{4,0},{8,12},{12,8},{16,20},{20,16},{24,28},{28,24},{1,5},{5... | collective-permute-start | bytes 3145736 | tf_op jit(solution)/shard_map/ppermute | solution.py:52
  220.3 41.6 %collective-permute-start.58 = (bf16[4,128,1024]{2,1,0:T(8,128)(2,1)}, bf16[4,128,1024]{2,1,0:T(8,128)(2,1)}, u32[]{:S(2)}, u32[]{:S(2)}) collective-permute-start(bf16[4,128,1024]{2,1,0:T(8,128)(2,1)} %fusion.58), channel_id=1, source_target_pairs={{0,4},{4,0},{8,12},{12,8},{16,20},{20,16},{24,28},{28,24},{1,5},{5... | collective-permute-start | bytes 3145736 | tf_op jit(solution)/shard_map/ppermute | solution.py:52
  247.9 21.9 %collective-permute-start.28 = (bf16[2,256,1024]{2,1,0:T(8,128)(2,1)S(1)}, bf16[2,256,1024]{2,1,0:T(8,128)(2,1)}, u32[]{:S(2)}, u32[]{:S(2)}) collective-permute-start(bf16[2,256,1024]{2,1,0:T(8,128)(2,1)S(1)} %fusion.60), channel_id=1, source_target_pairs={{0,1},{1,0},{2,3},{3,2},{4,5},{5,4},{6,7},{7,6},{8,9},{9,8},{10,11... | collective-permute-start | bytes 3145736 | tf_op jit(solution)/shard_map/ppermute | solution.py:62
  261.4 25.4 %collective-permute-start.54 = (bf16[4,128,1024]{2,1,0:T(8,128)(2,1)S(1)}, bf16[4,128,1024]{2,1,0:T(8,128)(2,1)S(1)}, u32[]{:S(2)}, u32[]{:S(2)}) collective-permute-start(bf16[4,128,1024]{2,1,0:T(8,128)(2,1)S(1)} %fusion.57), channel_id=1, source_target_pairs={{0,4},{4,0},{8,12},{12,8},{16,20},{20,16},{24,28},{28,24},{1,5},{5... | collective-permute-start | bytes 3145736 | tf_op jit(solution)/shard_map/ppermute | solution.py:52
  263.7 41.5 %collective-permute-start.59 = (bf16[128,1024]{1,0:T(8,128)(2,1)S(1)}, bf16[128,1024]{1,0:T(8,128)(2,1)S(1)}, u32[]{:S(2)}, u32[]{:S(2)}) collective-permute-start(bf16[128,1024]{1,0:T(8,128)(2,1)S(1)} %get-tuple-element.63), channel_id=1, source_target_pairs={{0,8},{4,12},{8,16},{12,20},{16,24},{20,28},{24,0},{28,4},{1,9},{5... | collective-permute-start | bytes 786440 | tf_op jit(solution)/shard_map/ppermute | solution.py:52
  265.7 39.6 %collective-permute-start.60 = (bf16[128,1024]{1,0:T(8,128)(2,1)S(1)}, bf16[128,1024]{1,0:T(8,128)(2,1)S(1)}, u32[]{:S(2)}, u32[]{:S(2)}) collective-permute-start(bf16[128,1024]{1,0:T(8,128)(2,1)S(1)} %get-tuple-element.65), channel_id=1, source_target_pairs={{0,16},{4,20},{8,24},{12,28},{16,0},{20,4},{24,8},{28,12},{1,17},{... | collective-permute-start | bytes 786440 | tf_op jit(solution)/shard_map/ppermute | solution.py:52
  269.2 39.2 %collective-permute-start.61 = (bf16[128,1024]{1,0:T(8,128)(2,1)S(1)}, bf16[128,1024]{1,0:T(8,128)(2,1)}, u32[]{:S(2)}, u32[]{:S(2)}) collective-permute-start(bf16[128,1024]{1,0:T(8,128)(2,1)S(1)} %get-tuple-element.64), channel_id=1, source_target_pairs={{0,24},{4,28},{8,0},{12,4},{16,8},{20,12},{24,16},{28,20},{1,25},{... | collective-permute-start | bytes 786440 | tf_op jit(solution)/shard_map/ppermute | solution.py:52
  269.8 19.2 %collective-permute-start.34 = (bf16[256,1024]{1,0:T(8,128)(2,1)S(1)}, bf16[256,1024]{1,0:T(8,128)(2,1)S(1)}, u32[]{:S(2)}, u32[]{:S(2)}) collective-permute-start(bf16[256,1024]{1,0:T(8,128)(2,1)S(1)} %fusion.70), channel_id=1, source_target_pairs={{0,2},{1,3},{2,0},{3,1},{4,6},{5,7},{6,4},{7,5},{8,10},{9,11},{10,... | collective-permute-start | bytes 1572872 | tf_op jit(solution)/shard_map/ppermute | solution.py:62
  289.0 21.9 %collective-permute-start.55 = (bf16[128,1024]{1,0:T(8,128)(2,1)}, bf16[128,1024]{1,0:T(8,128)(2,1)}, u32[]{:S(2)}, u32[]{:S(2)}) collective-permute-start(bf16[128,1024]{1,0:T(8,128)(2,1)} %get-tuple-element.66), channel_id=1, source_target_pairs={{0,8},{4,12},{8,16},{12,20},{16,24},{20,28},{24,0},{28,4},{1,9},{5... | collective-permute-start | bytes 786440 | tf_op jit(solution)/shard_map/ppermute | solution.py:52
  366.0 26.9 %collective-permute-start.46 = (bf16[4,128,768]{2,1,0:T(8,128)(2,1)S(1)}, bf16[4,128,768]{2,1,0:T(8,128)(2,1)S(1)}, u32[]{:S(2)}, u32[]{:S(2)}) collective-permute-start(bf16[4,128,768]{2,1,0:T(8,128)(2,1)S(1)} %fusion.66), channel_id=1, source_target_pairs={{0,4},{4,0},{8,12},{12,8},{16,20},{20,16},{24,28},{28,24},{1,5},{5... | collective-permute-start | bytes 2359304 | tf_op jit(solution)/shard_map/ppermute | solution.py:52
  371.4 34.6 %collective-permute-start.51 = (bf16[32,1024]{1,0:T(8,128)(2,1)S(1)}, bf16[32,1024]{1,0:T(8,128)(2,1)S(1)}, u32[]{:S(2)}, u32[]{:S(2)}) collective-permute-start(bf16[32,1024]{1,0:T(8,128)(2,1)S(1)} %get-tuple-element.81), channel_id=1, source_target_pairs={{0,8},{4,12},{8,16},{12,20},{16,24},{20,28},{24,0},{28,4},{1,9},{5... | collective-permute-start | bytes 196616 | tf_op jit(solution)/shard_map/ppermute | solution.py:52
  371.5 34.8 %collective-permute-start.52 = (bf16[32,1024]{1,0:T(8,128)(2,1)S(1)}, bf16[32,1024]{1,0:T(8,128)(2,1)S(1)}, u32[]{:S(2)}, u32[]{:S(2)}) collective-permute-start(bf16[32,1024]{1,0:T(8,128)(2,1)S(1)} %get-tuple-element.83), channel_id=1, source_target_pairs={{0,16},{4,20},{8,24},{12,28},{16,0},{20,4},{24,8},{28,12},{1,17},{... | collective-permute-start | bytes 196616 | tf_op jit(solution)/shard_map/ppermute | solution.py:52
  (92 other events, 755.9 us)

commit v2 on v1

--- a/solution.py
+++ b/solution.py
@@ -1,6 +1,10 @@
+import functools
+
 import jax
 import jax.numpy as jnp
 from jax import lax
+from jax.experimental import pallas as pl
+from jax.experimental.pallas import tpu as pltpu
 from jax.sharding import PartitionSpec as P
 
 HD = 64
@@ -158,66 +162,105 @@
     )
 
 
-def block_scores(queries, keys_all, seq_ids, places, start, block, factor):
-    query_blk = queries[start : start + block]
-    scores = (
-        jnp.einsum("qhd,khd->hqk", query_blk, keys_all, preferred_element_type=jnp.float32) * factor
-    )
-    allowed = (seq_ids[start : start + block, None] == seq_ids[None, :]) & (
-        places[None, :] <= places[start : start + block, None]
-    )
-    return jnp.where(allowed[None], scores, -1000000000.0)
-
-
-def attend(queries, keys_all, values_all, seq_ids, block, factor):
-    places = jnp.arange(keys_all.shape[0], dtype=jnp.int32)
-    outputs = []
-    totals = []
-    for start in range(0, keys_all.shape[0], block):
-        scores = block_scores(queries, keys_all, seq_ids, places, start, block, factor)
-        top = jnp.max(scores, axis=-1, keepdims=True)
-        expo = jnp.exp(scores - top)
-        summed = jnp.sum(expo, axis=-1, keepdims=True)
-        probs_low = (expo / summed).astype(jnp.bfloat16)
-        outputs.append(
-            jnp.einsum("hqk,khd->qhd", probs_low, values_all, preferred_element_type=jnp.float32)
-        )
-        totals.append(top + jnp.log(summed))
-    return (jnp.concatenate(outputs, 0), jnp.concatenate(totals, 1))
-
-
-def attend_back(queries, keys_all, values_all, grad_heads, seq_ids, log_sums, block, factor):
-    places = jnp.arange(keys_all.shape[0], dtype=jnp.int32)
-    query_grads = []
-    key_grad = jnp.zeros(keys_all.shape, jnp.float32)
-    value_grad = jnp.zeros(values_all.shape, jnp.float32)
-    for start in range(0, keys_all.shape[0], block):
-        scores = block_scores(queries, keys_all, seq_ids, places, start, block, factor)
-        probs = jnp.exp(scores - log_sums[:, start : start + block])
-        grad_blk = grad_heads[start : start + block]
-        grad_probs = jnp.einsum(
-            "qhd,khd->hqk", grad_blk, values_all, preferred_element_type=jnp.float32
-        )
-        delta = jnp.sum(probs * grad_probs, axis=-1, keepdims=True)
-        grad_scores = (probs * (grad_probs - delta)).astype(jnp.bfloat16)
-        query_grads.append(
-            jnp.einsum("hqk,khd->qhd", grad_scores, keys_all, preferred_element_type=jnp.float32)
-            * factor
-        )
-        key_grad = (
-            key_grad
-            + jnp.einsum(
-                "hqk,qhd->khd",
-                grad_scores,
-                queries[start : start + block],
-                preferred_element_type=jnp.float32,
+BLOCK = 256
+MASKED = -1000000000.0
+
+
+def masked_scores(queries, keys, ids_row_ref, ids_col_ref, start, stop):
+    scores = contract_cols(keys, queries)
+    same = ids_col_ref[:stop, :] == ids_row_ref[:, start:stop]
+    key_place = lax.broadcasted_iota(jnp.int32, scores.shape, 0)
+    query_place = lax.broadcasted_iota(jnp.int32, scores.shape, 1) + start
+    return jnp.where(same & (key_place <= query_place), scores, MASKED)
+
+
+def attend_kernel(heads, block, factor, qkv_ref, ids_row_ref, ids_col_ref, out_ref, lse_ref):
+    rows = qkv_ref.shape[0]
+    width = heads * HD
+    for start in range(0, rows, block):
+        stop = start + block
+        for head in range(heads):
+            lo, hi = head * HD, (head + 1) * HD
+            queries = qkv_ref[start:stop, lo:hi] * jnp.asarray(factor, jnp.bfloat16)
+            keys = qkv_ref[:stop, width + lo : width + hi]
+            values = qkv_ref[:stop, 2 * width + lo : 2 * width + hi]
+            scores = masked_scores(queries, keys, ids_row_ref, ids_col_ref, start, stop)
+            top = jnp.max(scores, axis=0, keepdims=True)
+            expo = jnp.exp(scores - top)
+            summed = jnp.sum(expo, axis=0, keepdims=True)
+            probs_low = (expo * (1.0 / summed)).astype(jnp.bfloat16)
+            out_ref[start:stop, lo:hi] = contract_rows(values, probs_low).T.astype(jnp.bfloat16)
+            lse_ref[head : head + 1, start:stop] = top + jnp.log(summed)
+
+
+def attend_back_kernel(
+    heads, block, factor, qkv_ref, grad_ref, lse_ref, ids_row_ref, ids_col_ref, out_ref, key_acc, value_acc
+):
+    rows = qkv_ref.shape[0]
+    width = heads * HD
+    for head in range(heads):
+        lo, hi = head * HD, (head + 1) * HD
+        for start in reversed(range(0, rows, block)):
+            stop = start + block
+            queries = qkv_ref[start:stop, lo:hi] * jnp.asarray(factor, jnp.bfloat16)
+            keys = qkv_ref[:stop, width + lo : width + hi]
+            values = qkv_ref[:stop, 2 * width + lo : 2 * width + hi]
+            grads = grad_ref[start:stop, lo:hi]
+            scores = masked_scores(queries, keys, ids_row_ref, ids_col_ref, start, stop)
+            probs = jnp.exp(scores - lse_ref[head : head + 1, start:stop])
+            grad_probs = contract_cols(values, grads)
+            delta = jnp.sum(probs * grad_probs, axis=0, keepdims=True)
+            grad_scores = (probs * (grad_probs - delta)).astype(jnp.bfloat16)
+            query_grad = contract_rows(keys, grad_scores).T * factor
+            out_ref[start:stop, lo:hi] = query_grad.astype(jnp.bfloat16)
+            key_grad = jnp.dot(grad_scores, queries, preferred_element_type=jnp.float32)
+            value_grad = jnp.dot(
+                probs.astype(jnp.bfloat16), grads, preferred_element_type=jnp.float32
             )
-            * factor
-        )
-        value_grad = value_grad + jnp.einsum(
-            "hqk,qhd->khd", probs.astype(jnp.bfloat16), grad_blk, preferred_element_type=jnp.float32
-        )
-    return (jnp.concatenate(query_grads, 0), key_grad, value_grad)
+            if stop == rows:
+                key_acc[...] = key_grad
+                value_acc[...] = value_grad
+            else:
+                key_acc[:stop, :] += key_grad
+                value_acc[:stop, :] += value_grad
+        out_ref[:, width + lo : width + hi] = key_acc[...].astype(jnp.bfloat16)
+        out_ref[:, 2 * width + lo : 2 * width + hi] = value_acc[...].astype(jnp.bfloat16)
+
+
+def attend(qkv, seq_ids, heads, factor):
+    rows = qkv.shape[0]
+    block = min(BLOCK, rows)
+    return pl.pallas_call(
+        functools.partial(attend_kernel, heads, block, factor),
+        out_shape=(
+            jax.ShapeDtypeStruct((rows, heads * HD), jnp.bfloat16),
+            jax.ShapeDtypeStruct((heads, rows), jnp.float32),
+        ),
+        compiler_params=pltpu.CompilerParams(vmem_limit_bytes=40 * 2**20),
+        cost_estimate=pl.CostEstimate(
+            flops=4 * rows * rows * 256 * heads,
+            bytes_accessed=8 * rows * heads * HD,
+            transcendentals=rows * rows * heads,
+        ),
+        name="attend",
+    )(qkv, seq_ids[None, :], seq_ids[:, None])
+
+
+def attend_back(qkv, grads, log_sums, seq_ids, heads, factor):
+    rows = qkv.shape[0]
+    block = min(BLOCK, rows)
+    return pl.pallas_call(
+        functools.partial(attend_back_kernel, heads, block, factor),
+        out_shape=jax.ShapeDtypeStruct(qkv.shape, jnp.bfloat16),
+        scratch_shapes=[pltpu.VMEM((rows, HD), jnp.float32)] * 2,
+        compiler_params=pltpu.CompilerParams(vmem_limit_bytes=40 * 2**20),
+        cost_estimate=pl.CostEstimate(
+            flops=10 * rows * rows * 256 * heads,
+            bytes_accessed=14 * rows * heads * HD,
+            transcendentals=rows * rows * heads,
+        ),
+        name="attend_back",
+    )(qkv, grads, log_sums, seq_ids[None, :], seq_ids[:, None])
 
 
 def on_device(
@@ -260,20 +303,28 @@
     heads_here = width // HD
     hidden_here = up_weight.shape[1]
     factor = 1.0 / HD**0.5
-    block = min(512, capacity)
     group_ids = doc_ids[0]
     own_ids = lax.dynamic_slice_in_dim(group_ids, place * rows, rows)
     input_all = gather_rows(block_input)
-    small_all = gather_weight(small.reshape(-1, 128)).reshape(shards, small.shape[0])
+    qkv_rows = qkv_weight.shape[0]
+    small_rows = -(-small.shape[0] // (3 * width * 16)) * 16
+    first = jnp.concatenate(
+        [
+            qkv_weight.reshape(qkv_rows, 3 * width),
+            jnp.pad(small, (0, small_rows * 3 * width - small.shape[0])).reshape(
+                small_rows, 3 * width
+            ),
+        ]
+    )
+    first_all = gather_weight(first)
+    small_all = first_all[:, qkv_rows:].reshape(shards, -1)[:, : small.shape[0]]
     piece = model // shards
     gain_one, shift_one, query_shift, value_shift, out_shift, gain_two, shift_two, down_shift = (
         small_all[:, i * piece : (i + 1) * piece].reshape(model) for i in range(8)
     )
     up_shift = small_all[:, 8 * piece :].reshape(-1)
     qv_full = jnp.stack([query_shift, value_shift])
-    qkv_flat = gather_weight(qkv_weight.reshape(qkv_weight.shape[0], 3 * width)).reshape(
-        model, 3 * width
-    )
+    qkv_flat = first_all[:, :qkv_rows].reshape(model, 3 * width)
     out_full = gather_weight(out_weight).reshape(width, model)
     up_full = gather_weight(up_weight).reshape(model, hidden_here)
     down_full = gather_weight(down_weight).reshape(hidden_here, model)
@@ -284,17 +335,11 @@
         up_shift.astype(jnp.float32), place * hidden_here, hidden_here, 0
     )
     input_float = block_input.astype(jnp.float32)
-    norm_one = normalize(input_float)
-    h_one_all = (normalize(input_all.astype(jnp.float32)) * gain_one + shift_one).astype(
-        jnp.bfloat16
-    )
+    norm_one_all = normalize(input_all.astype(jnp.float32))
+    h_one_all = (norm_one_all * gain_one + shift_one).astype(jnp.bfloat16)
     qkv_proj = project(h_one_all, qkv_flat)
-    qkv = (qkv_proj + qkv_shift).astype(jnp.bfloat16).reshape(capacity, 3, heads_here, HD)
-    queries = qkv[:, 0]
-    keys_all = qkv[:, 1]
-    values_all = qkv[:, 2]
-    attended, log_sums = attend(queries, keys_all, values_all, group_ids, block, factor)
-    mixed_all = attended.astype(jnp.bfloat16).reshape(capacity, width)
+    qkv = (qkv_proj + qkv_shift).astype(jnp.bfloat16)
+    mixed_all, log_sums = attend(qkv, group_ids, heads_here, factor)
     out_part = project(mixed_all, out_full)
     resid = input_float + reduce_rows(out_part) + out_shift
     norm_two = normalize(resid)
@@ -328,26 +373,18 @@
     out_shift_grad = jnp.sum(resid_low.astype(jnp.float32), axis=0)
     resid_all = gather_rows(resid_low)
     out_grad = weight_grad(mixed_all, resid_all)
-    grad_heads = (
-        project_back(resid_all, out_full).astype(jnp.bfloat16).reshape(capacity, heads_here, HD)
-    )
-    query_grad, key_grad, value_grad = attend_back(
-        queries, keys_all, values_all, grad_heads, group_ids, log_sums, block, factor
-    )
-    grad_qkv = (
-        jnp.stack([query_grad, key_grad, value_grad], 1)
-        .astype(jnp.bfloat16)
-        .reshape(capacity, 3 * width)
-    )
+    grad_heads = project_back(resid_all, out_full).astype(jnp.bfloat16)
+    grad_qkv = attend_back(qkv, grad_heads, log_sums, group_ids, heads_here, factor)
     qkv_grad = weight_grad(h_one_all, grad_qkv).reshape(qkv_weight.shape[0], 3, width)
     column_sums = jnp.sum(grad_qkv.astype(jnp.float32), axis=0).reshape(3, width)
     qv_local = jnp.stack([column_sums[0], column_sums[2]])
     qv_grad = lax.dynamic_update_slice_in_dim(
         jnp.zeros((2, model), jnp.float32), qv_local, place * width, 1
     )
-    grad_h_one = reduce_rows(project_back(grad_qkv, qkv_flat))
-    gain_one_grad = jnp.sum(grad_h_one * norm_one, axis=0)
-    shift_one_grad = jnp.sum(grad_h_one, axis=0)
+    grad_h_one_part = project_back(grad_qkv, qkv_flat)
+    gain_one_grad = jnp.sum(grad_h_one_part * norm_one_all, axis=0)
+    shift_one_grad = jnp.sum(grad_h_one_part, axis=0)
+    grad_h_one = reduce_rows(grad_h_one_part)
     unused_one, norm_back_one = jax.vjp(normalize, input_float)
     input_grad = grad_resid + norm_back_one(grad_h_one * gain_one.astype(jnp.float32))[0]
     packed = jnp.concatenate(

time: 429 us -> 410 us (0.956)
  waiting for transfers between devices: 116 us -> 154 us
  matrix products: 73.2 us -> 44.8 us
  Pallas kernels: 0 us -> 20.9 us
  local copies, waits for them, and re-layouts: 109 us -> 89.7 us
  starting transfers between devices: 73.5 us -> 55 us
  other arithmetic: 48.6 us -> 36.1 us
    ppermute x40 -> x36, waiting for transfers between devices: 74.3 us -> 120 us  [move_fsdp(): return lax.ppermute(values, 'fsdp', pairs)]
    dot_general x12 -> x0, matrix products: 28.2 us -> none  [the longest x2 6.33 us: attend_back(): jnp.einsum('hqk,khd->qhd', grad_scores, keys_all, preferred_element_type=...]
    pallas_call x0 -> x2, Pallas kernels: none -> 20.9 us  [the longest x1 11.5 us: attend_back(): pl.pallas_call(functools.partial(attend_back_kernel, heads, block, factor...]
    ppermute x40 -> x36, starting transfers between devices: 64.4 us -> 46.2 us  [move_fsdp(): return lax.ppermute(values, 'fsdp', pairs)]
    unnamed x128 -> x115, local copies, waits for them, and re-layouts: 30.8 us -> 20.1 us
    ppermute x22, waiting for transfers between devices: 41.7 us -> 33.8 us  [move_ctx(): return lax.ppermute(values, 'ctx', pairs)]
    convert_element_type x2 -> x0, local copies, waits for them, and re-layouts: 5.57 us -> none  [the longest x1 3.01 us: on_device(): input_all.astype(jnp.float32)]
    dot_general x1 -> x3, local copies, waits for them, and re-layouts: 3.97 us -> 8.9 us  [contract_rows(): lax.dot_general(left, right, (((0,), (0,)), ((), ())), preferred_element_...]
  transfers between devices with their start and end apart: 62 -> 58, of which waited for: 24 -> 23; matrix products, arithmetic and copies ran while one was open for 36% -> 33% of each run, Pallas kernels for 0% -> 5%
where the time goes in v2:
time: 410 us; the launch traced here: 403 us
  waiting for transfers between devices  154 us (38%)
  local copies, waits for them, and re-layouts  89.7 us (22%)
  starting transfers between devices  55 us (13%)
  matrix products  44.8 us (11%)
  other arithmetic  36.1 us (9%)
  Pallas kernels  20.9 us (5%)
    ppermute x36, waiting for transfers between devices, move_fsdp(): return lax.ppermute(values, 'fsdp', pairs)  120 us
    ppermute x36, starting transfers between devices, move_fsdp(): return lax.ppermute(values, 'fsdp', pairs)  46.2 us
    ppermute x22, waiting for transfers between devices, move_ctx(): return lax.ppermute(values, 'ctx', pairs)  33.8 us
    dynamic_update_slice x30, local copies, waits for them, and re-layouts, put(): return lax.dynamic_update_index_in_dim(buffer, values, place, axis)  21.9 us
    dot_general x4, matrix products, contract_cols(): lax.dot_general(left, right, (((1,), (1,)), ((), ())), preferred_element_...  20.8 us
    unnamed x115, local copies, waits for them, and re-layouts  20.1 us
    dot_general x4, matrix products, project(): return jnp.dot(inputs, weight, preferred_element_type=jnp.float32)  15.1 us
    pallas_call x1, Pallas kernels, attend_back(): pl.pallas_call(functools.partial(attend_back_kernel, heads, block, factor...  11.5 us
  transfers between devices with their start and end apart: 58, of which 23 were waited for; matrix products, arithmetic and copies ran while one was open for 33% of the time, Pallas kernels for 5%

profile of v2, /device:TPU:8, one launch (start us, length us, event | category | flops | bytes accessed | tf_op | source)
XLA Modules:
  0.0 402.8 jit_solution(5449021621328186205)
XLA Ops:
  28.5 15.1 %collective-permute-done.9 = bf16[32,1024]{1,0:T(8,128)(2,1)S(1)} collective-permute-done((bf16[32,1024]{1,0:T(8,128)(2,1)}, bf16[32,1024]{1,0:T(8,128)(2,1)S(1)}, u32[]{:S(2)}, u32[]{:S(2)}) %collective-permute-start.9) | collective-permute-done | bytes 65568 | tf_op jit(solution)/shard_map/ppermute | solution.py:56
  48.5 15.4 %collective-permute-done.5 = bf16[144,768]{0,1:T(8,128)(2,1)} collective-permute-done((bf16[144,768]{0,1:T(8,128)(2,1)}, bf16[144,768]{0,1:T(8,128)(2,1)}, u32[]{:S(2)}, u32[]{:S(2)}) %collective-permute-start.5) | collective-permute-done | bytes 221216 | tf_op jit(solution)/shard_map/ppermute | solution.py:56
  83.1 14.5 %collective-permute-done.6 = bf16[4,144,768]{2,1,0:T(8,128)(2,1)S(1)} collective-permute-done((bf16[4,144,768]{2,1,0:T(8,128)(2,1)S(1)}, bf16[4,144,768]{2,1,0:T(8,128)(2,1)S(1)}, u32[]{:S(2)}, u32[]{:S(2)}) %collective-permute-start.6) | collective-permute-done | bytes 884768 | tf_op jit(solution)/shard_map/ppermute | solution.py:56
  103.1 9.4 %attend.1 = (bf16[1024,256]{1,0:T(8,128)(2,1)S(1)}, f32[4,1024]{1,0:T(4,128)S(1)}) custom-call(bf16[1024,768]{1,0:T(8,128)(2,1)S(1)} %add_convert_fusion.2.qkv_ref, s32[1,1024]{1,0:T(1,128)S(1)} %copy-done, s32[1024,1]{1,0:T(8,128)S(1)} %copy.90.ids_col_ref), custom_call_target="tpu_custom_call" | custom-call | flops 4294967296 | bytes 2097152 | tf_op jit(solution)/shard_map/attend/pallas_call | solution.py:233
  121.2 14.3 %collective-permute-done.21 = bf16[128,1024]{1,0:T(8,128)(2,1)S(1)} collective-permute-done((bf16[128,1024]{1,0:T(8,128)(2,1)S(1)}, bf16[128,1024]{1,0:T(8,128)(2,1)S(1)}, u32[]{:S(2)}, u32[]{:S(2)}) %collective-permute-start.21) | collective-permute-done | bytes 262176 | tf_op jit(solution)/shard_map/ppermute | solution.py:56
  145.2 10.1 %collective-permute-done.12 = bf16[256,1024]{1,0:T(8,128)(2,1)S(1)} collective-permute-done((bf16[256,1024]{1,0:T(8,128)(2,1)S(1)}, bf16[256,1024]{1,0:T(8,128)(2,1)S(1)}, u32[]{:S(2)}, u32[]{:S(2)}) %collective-permute-start.12) | collective-permute-done | bytes 524320 | tf_op jit(solution)/shard_map/ppermute | solution.py:66
  163.8 19.6 %collective-permute-done.23 = bf16[4,128,1024]{2,1,0:T(8,128)(2,1)} collective-permute-done((bf16[4,128,1024]{2,1,0:T(8,128)(2,1)}, bf16[4,128,1024]{2,1,0:T(8,128)(2,1)}, u32[]{:S(2)}, u32[]{:S(2)}) %collective-permute-start.23) | collective-permute-done | bytes 1048608 | tf_op jit(solution)/shard_map/ppermute | solution.py:56
  192.0 3.9 copy.112
  195.9 8.0 %fusion.10 = (bf16[1024,1024]{0,1:T(8,128)(2,1)}, f32[1024,1024]{1,0:T(8,128)}) fusion(f32[1024]{0:T(1024)S(1)} %dynamic_slice.162, bf16[1024,1024]{1,0:T(8,128)(2,1)} %bitcast.44, bf16[1024,1024]{1,0:T(8,128)(2,1)} %bitcast.425), kind=kOutput, calls=%fused_computation.15 | convolution fusion | flops 2157969408 | bytes 10489856 | tf_op jit(solution)/shard_map/dot_general | solution.py:150
  217.1 5.4 %copy.93 = f32[1024,1024]{0,1:T(8,128)} copy(f32[1024,1024]{1,0:T(8,128)} %get-tuple-element.140) | data formatting | bytes 8388608 | tf_op jit(solution)/shard_map/add | solution.py:349
  222.5 10.0 %convert_reduce_fusion = (f32[1024]{0:T(1024)S(1)}, bf16[1024,1024]{0,1:T(8,128)(2,1)}, bf16[1024,1024]{0,1:T(8,128)(2,1)}) fusion(f32[1024,1024]{0,1:T(8,128)} %copy.93, bf16[1024,1024]{1,0:T(8,128)(2,1)} %bitcast.420, bf16[1024,1024]{1,0:T(8,128)(2,1)} %bitcast.427), kind=kOutput, calls=%fused_computation.20 | convolution fusion | flops 2176842752 | bytes 12587008 | tf_op jit(solution)/shard_map/dot_general | solution.py:38
  232.5 4.0 copy.124
  236.5 4.5 %fusion.92 = f32[2,2,256,1024]{3,2,1,0:T(8,128)S(1)} fusion(bf16[2,2,256,1024]{3,2,1,0:T(8,128)(2,1)} %bitcast.433, bf16[1024,1024,1,1]{1,0,3,2:T(8,128)(2,1)} %bitcast.428), kind=kOutput, calls=%fused_computation.261 | convolution fusion | flops 2147483648 | bytes 8388608 | tf_op jit(solution)/shard_map/dot_general | solution.py:150
  243.5 4.3 %copy.125 = bf16[1024,1024]{1,0:T(8,128)(2,1)} copy(bf16[1024,1024]{0,1:T(8,128)(2,1)} %get-tuple-element.68) | data formatting | bytes 4194304 | tf_op jit(solution)/shard_map/dot_general | solution.py:38
  247.9 4.7 %fusion.93 = f32[2,2,256,1024]{3,2,1,0:T(8,128)S(1)} fusion(bf16[2,2,256,1024]{3,2,1,0:T(8,128)(2,1)} %bitcast.435, bf16[1024,1024,1,1]{1,0,3,2:T(8,128)(2,1)} %bitcast.426), kind=kOutput, calls=%fused_computation.262 | convolution fusion | flops 2147483648 | bytes 8388608 | tf_op jit(solution)/shard_map/dot_general | solution.py:38
  267.5 14.7 %collective-permute-done.50 = bf16[4,128,1024]{2,1,0:T(8,128)(2,1)S(1)} collective-permute-done((bf16[4,128,1024]{2,1,0:T(8,128)(2,1)S(1)}, bf16[4,128,1024]{2,1,0:T(8,128)(2,1)S(1)}, u32[]{:S(2)}, u32[]{:S(2)}) %collective-permute-start.50) | collective-permute-done | bytes 1048608 | tf_op jit(solution)/shard_map/ppermute | solution.py:56
  284.8 10.8 %collective-permute-done.25 = bf16[256,1024]{1,0:T(8,128)(2,1)S(1)} collective-permute-done((bf16[256,1024]{1,0:T(8,128)(2,1)S(1)}, bf16[256,1024]{1,0:T(8,128)(2,1)S(1)}, u32[]{:S(2)}, u32[]{:S(2)}) %collective-permute-start.25) | collective-permute-done | bytes 524320 | tf_op jit(solution)/shard_map/ppermute | solution.py:66
  305.2 3.9 collective-permute-done.52
  319.5 11.5 %attend_back.1 = bf16[1024,768]{1,0:T(8,128)(2,1)S(1)} custom-call(bf16[1024,768]{1,0:T(8,128)(2,1)S(1)} %copy-done.2, bf16[1024,256]{1,0:T(8,128)(2,1)S(1)} %convolution_convert_fusion.grad_ref, f32[4,1024]{1,0:T(4,128)S(1)} %get-tuple-element.17.lse_ref, s32[1,1024]{1,0:T(1,128)S(1)} %copy-done, s32[1024,1]{1,0:T(8,128)S(1)} %copy.90.ids_col_ref), custom_call_target="tpu_custom_call" | custom-call | flops 10737418240 | bytes 3670016 | tf_op jit(solution)/shard_map/attend_back/pallas_call | solution.py:252
  331.3 5.3 %fusion.81 = (f32[1024]{0:T(1024)S(1)}, f32[1024]{0:T(1024)S(1)}, bf16[1024,1024]{1,0:T(8,128)(2,1)}, f32[1024,1024]{1,0:T(8,128)}) fusion(f32[1024]{0:T(1024)S(1)} %bitcast.451, f32[1024]{0:T(1024)S(1)} %bitcast.452, bf16[4,256,1024]{2,1,0:T(8,128)(2,1)} %bitcast_dynamic-update-slice_fusion.12, f32[1024]{0:T(1024)S(1)} %get-tuple-element.113, ...), kind=kOutput, calls=%fused_computation.253 | convolution fusion | flops 1620047872 | bytes 11558912 | tf_op jit(solution)/shard_map/dot_general | solution.py:38
  336.6 4.0 copy.126
  356.4 9.8 %collective-permute-done.35 = bf16[256,1024]{1,0:T(8,128)(2,1)S(1)} collective-permute-done((bf16[256,1024]{1,0:T(8,128)(2,1)S(1)}, bf16[256,1024]{1,0:T(8,128)(2,1)S(1)}, u32[]{:S(2)}, u32[]{:S(2)}) %collective-permute-start.35) | collective-permute-done | bytes 524320 | tf_op jit(solution)/shard_map/ppermute | solution.py:66
  385.5 4.1 %collective-permute-done.49 = bf16[32,1024]{1,0:T(8,128)(2,1)S(1)} collective-permute-done((bf16[32,1024]{1,0:T(8,128)(2,1)S(1)}, bf16[32,1024]{1,0:T(8,128)(2,1)S(1)}, u32[]{:S(2)}, u32[]{:S(2)}) %collective-permute-start.49) | collective-permute-done | bytes 65568 | tf_op jit(solution)/shard_map/ppermute | solution.py:56
  390.8 4.5 %collective-permute-done.43 = bf16[128,768]{1,0:T(8,128)(2,1)S(1)} collective-permute-done((bf16[128,768]{1,0:T(8,128)(2,1)S(1)}, bf16[128,768]{1,0:T(8,128)(2,1)S(1)}, u32[]{:S(2)}, u32[]{:S(2)}) %collective-permute-start.43) | collective-permute-done | bytes 196640 | tf_op jit(solution)/shard_map/ppermute | solution.py:56
  (368 shorter events, 188.5 us)
Async XLA Ops:
  0.7 65.9 %collective-permute-start.16 = (bf16[128,1024]{1,0:T(8,128)(2,1)}, bf16[128,1024]{1,0:T(8,128)(2,1)}, u32[]{:S(2)}, u32[]{:S(2)}) collective-permute-start(bf16[128,1024]{1,0:T(8,128)(2,1)} %param.24), channel_id=1, source_target_pairs={{0,8},{4,12},{8,16},{12,20},{16,24},{20,28},{24,0},{28,4},{1,9},{5... | collective-permute-start | bytes 786440 | tf_op jit(solution)/shard_map/ppermute | solution.py:56
  2.4 111.1 %collective-permute-start.17 = (bf16[128,1024]{1,0:T(8,128)(2,1)}, bf16[128,1024]{1,0:T(8,128)(2,1)}, u32[]{:S(2)}, u32[]{:S(2)}) collective-permute-start(bf16[128,1024]{1,0:T(8,128)(2,1)} %param.24), channel_id=1, source_target_pairs={{0,16},{4,20},{8,24},{12,28},{16,0},{20,4},{24,8},{28,12},{1,17},{... | collective-permute-start | bytes 786440 | tf_op jit(solution)/shard_map/ppermute | solution.py:56
  4.3 22.5 %collective-permute-start.8 = (bf16[32,1024]{1,0:T(8,128)(2,1)}, bf16[32,1024]{1,0:T(8,128)(2,1)S(1)}, u32[]{:S(2)}, u32[]{:S(2)}) collective-permute-start(bf16[32,1024]{1,0:T(8,128)(2,1)} %param.20), channel_id=1, source_target_pairs={{0,16},{4,20},{8,24},{12,28},{16,0},{20,4},{24,8},{28,12},{1,17},{... | collective-permute-start | bytes 196616 | tf_op jit(solution)/shard_map/ppermute | solution.py:56
  7.8 35.8 %collective-permute-start.9 = (bf16[32,1024]{1,0:T(8,128)(2,1)}, bf16[32,1024]{1,0:T(8,128)(2,1)S(1)}, u32[]{:S(2)}, u32[]{:S(2)}) collective-permute-start(bf16[32,1024]{1,0:T(8,128)(2,1)} %param.20), channel_id=1, source_target_pairs={{0,24},{4,28},{8,0},{12,4},{16,8},{20,12},{24,16},{28,20},{1,25},{... | collective-permute-start | bytes 196616 | tf_op jit(solution)/shard_map/ppermute | solution.py:56
  43.9 71.3 %collective-permute-start.18 = (bf16[128,1024]{1,0:T(8,128)(2,1)}, bf16[128,1024]{1,0:T(8,128)(2,1)}, u32[]{:S(2)}, u32[]{:S(2)}) collective-permute-start(bf16[128,1024]{1,0:T(8,128)(2,1)} %param.24), channel_id=1, source_target_pairs={{0,24},{4,28},{8,0},{12,4},{16,8},{20,12},{24,16},{28,20},{1,25},{... | collective-permute-start | bytes 786440 | tf_op jit(solution)/shard_map/ppermute | solution.py:56
  45.8 25.6 %collective-permute-start.1 = (bf16[256,1024]{1,0:T(8,128)(2,1)S(1)}, bf16[256,1024]{1,0:T(8,128)(2,1)}, u32[]{:S(2)}, u32[]{:S(2)}) collective-permute-start(bf16[256,1024]{1,0:T(8,128)(2,1)S(1)} %copy-done.3), channel_id=1, source_target_pairs={{0,2},{1,3},{2,0},{3,1},{4,6},{5,7},{6,4},{7,5},{8,10},{9,11},{10,... | collective-permute-start | bytes 1572872 | tf_op jit(solution)/shard_map/ppermute | solution.py:66
  70.4 71.0 %collective-permute-start.26 = (bf16[256,1024]{1,0:T(8,128)(2,1)S(1)}, bf16[256,1024]{1,0:T(8,128)(2,1)S(1)}, u32[]{:S(2)}, u32[]{:S(2)}) collective-permute-start(bf16[256,1024]{1,0:T(8,128)(2,1)S(1)} %copy-done.8), channel_id=1, source_target_pairs={{0,1},{1,0},{2,3},{3,2},{4,5},{5,4},{6,7},{7,6},{8,9},{9,8},{10,11... | collective-permute-start | bytes 1572872 | tf_op jit(solution)/shard_map/ppermute | solution.py:66
  72.1 66.9 %collective-permute-start.27 = (bf16[256,1024]{1,0:T(8,128)(2,1)S(1)}, bf16[256,1024]{1,0:T(8,128)(2,1)}, u32[]{:S(2)}, u32[]{:S(2)}) collective-permute-start(bf16[256,1024]{1,0:T(8,128)(2,1)S(1)} %copy-done.8), channel_id=1, source_target_pairs={{0,2},{1,3},{2,0},{3,1},{4,6},{5,7},{6,4},{7,5},{8,10},{9,11},{10,... | collective-permute-start | bytes 1572872 | tf_op jit(solution)/shard_map/ppermute | solution.py:66
  97.7 22.5 %collective-permute-start.20 = (bf16[128,1024]{1,0:T(8,128)(2,1)S(1)}, bf16[128,1024]{1,0:T(8,128)(2,1)S(1)}, u32[]{:S(2)}, u32[]{:S(2)}) collective-permute-start(bf16[128,1024]{1,0:T(8,128)(2,1)S(1)} %copy-done.32), channel_id=1, source_target_pairs={{0,8},{4,12},{8,16},{12,20},{16,24},{20,28},{24,0},{28,4},{1,9},{5... | collective-permute-start | bytes 786440 | tf_op jit(solution)/shard_map/ppermute | solution.py:56
  113.4 25.5 %collective-permute-start.11 = (bf16[2,256,1024]{2,1,0:T(8,128)(2,1)S(1)}, bf16[2,256,1024]{2,1,0:T(8,128)(2,1)S(1)}, u32[]{:S(2)}, u32[]{:S(2)}) collective-permute-start(bf16[2,256,1024]{2,1,0:T(8,128)(2,1)S(1)} %fusion.22), channel_id=1, source_target_pairs={{0,1},{1,0},{2,3},{3,2},{4,5},{5,4},{6,7},{7,6},{8,9},{9,8},{10,11... | collective-permute-start | bytes 3145736 | tf_op jit(solution)/shard_map/ppermute | solution.py:66
  135.5 26.3 %collective-permute-start.19 = (bf16[4,128,1024]{2,1,0:T(8,128)(2,1)}, bf16[4,128,1024]{2,1,0:T(8,128)(2,1)}, u32[]{:S(2)}, u32[]{:S(2)}) collective-permute-start(bf16[4,128,1024]{2,1,0:T(8,128)(2,1)} %bitcast_dynamic-update-slice_fusion.20), channel_id=1, source_target_pairs={{0,4},{4,0},{8,12},{12,8},{16,20},{20,16},{24,28},{28,24},{1,5},{5... | collective-permute-start | bytes 3145736 | tf_op jit(solution)/shard_map/ppermute | solution.py:56
  138.5 44.9 %collective-permute-start.23 = (bf16[4,128,1024]{2,1,0:T(8,128)(2,1)}, bf16[4,128,1024]{2,1,0:T(8,128)(2,1)}, u32[]{:S(2)}, u32[]{:S(2)}) collective-permute-start(bf16[4,128,1024]{2,1,0:T(8,128)(2,1)} %bitcast_dynamic-update-slice_fusion.16), channel_id=1, source_target_pairs={{0,4},{4,0},{8,12},{12,8},{16,20},{20,16},{24,28},{28,24},{1,5},{5... | collective-permute-start | bytes 3145736 | tf_op jit(solution)/shard_map/ppermute | solution.py:56
  139.0 50.8 %collective-permute-start.28 = (bf16[256,1024]{1,0:T(8,128)(2,1)}, bf16[256,1024]{1,0:T(8,128)(2,1)}, u32[]{:S(2)}, u32[]{:S(2)}) collective-permute-start(bf16[256,1024]{1,0:T(8,128)(2,1)} %collective-permute-done.27), channel_id=1, source_target_pairs={{0,1},{1,0},{2,3},{3,2},{4,5},{5,4},{6,7},{7,6},{8,9},{9,8},{10,11... | collective-permute-start | bytes 1572872 | tf_op jit(solution)/shard_map/ppermute | solution.py:66
  160.8 24.3 %collective-permute-start.14 = (bf16[256,1024]{1,0:T(8,128)(2,1)S(1)}, bf16[256,1024]{1,0:T(8,128)(2,1)S(1)}, u32[]{:S(2)}, u32[]{:S(2)}) collective-permute-start(bf16[256,1024]{1,0:T(8,128)(2,1)S(1)} %get-tuple-element.76), channel_id=1, source_target_pairs={{0,2},{1,3},{2,0},{3,1},{4,6},{5,7},{6,4},{7,5},{8,10},{9,11},{10,... | collective-permute-start | bytes 1572872 | tf_op jit(solution)/shard_map/ppermute | solution.py:66
  163.5 24.6 %collective-permute-start.13 = (bf16[256,1024]{1,0:T(8,128)(2,1)S(1)}, bf16[256,1024]{1,0:T(8,128)(2,1)S(1)}, u32[]{:S(2)}, u32[]{:S(2)}) collective-permute-start(bf16[256,1024]{1,0:T(8,128)(2,1)S(1)} %get-tuple-element.76), channel_id=1, source_target_pairs={{0,1},{1,0},{2,3},{3,2},{4,5},{5,4},{6,7},{7,6},{8,9},{9,8},{10,11... | collective-permute-start | bytes 1572872 | tf_op jit(solution)/shard_map/ppermute | solution.py:66
  215.6 41.7 %collective-permute-start.54 = (bf16[4,128,1024]{2,1,0:T(8,128)(2,1)}, bf16[4,128,1024]{2,1,0:T(8,128)(2,1)}, u32[]{:S(2)}, u32[]{:S(2)}) collective-permute-start(bf16[4,128,1024]{2,1,0:T(8,128)(2,1)} %fusion.24), channel_id=1, source_target_pairs={{0,4},{4,0},{8,12},{12,8},{16,20},{20,16},{24,28},{28,24},{1,5},{5... | collective-permute-start | bytes 3145736 | tf_op jit(solution)/shard_map/ppermute | solution.py:56
  256.7 25.4 %collective-permute-start.50 = (bf16[4,128,1024]{2,1,0:T(8,128)(2,1)S(1)}, bf16[4,128,1024]{2,1,0:T(8,128)(2,1)S(1)}, u32[]{:S(2)}, u32[]{:S(2)}) collective-permute-start(bf16[4,128,1024]{2,1,0:T(8,128)(2,1)S(1)} %fusion.23), channel_id=1, source_target_pairs={{0,4},{4,0},{8,12},{12,8},{16,20},{20,16},{24,28},{28,24},{1,5},{5... | collective-permute-start | bytes 3145736 | tf_op jit(solution)/shard_map/ppermute | solution.py:56
  259.0 41.5 %collective-permute-start.55 = (bf16[128,1024]{1,0:T(8,128)(2,1)S(1)}, bf16[128,1024]{1,0:T(8,128)(2,1)S(1)}, u32[]{:S(2)}, u32[]{:S(2)}) collective-permute-start(bf16[128,1024]{1,0:T(8,128)(2,1)S(1)} %get-tuple-element.81), channel_id=1, source_target_pairs={{0,8},{4,12},{8,16},{12,20},{16,24},{20,28},{24,0},{28,4},{1,9},{5... | collective-permute-start | bytes 786440 | tf_op jit(solution)/shard_map/ppermute | solution.py:56
  259.1 41.5 %collective-permute-start.56 = (bf16[128,1024]{1,0:T(8,128)(2,1)S(1)}, bf16[128,1024]{1,0:T(8,128)(2,1)S(1)}, u32[]{:S(2)}, u32[]{:S(2)}) collective-permute-start(bf16[128,1024]{1,0:T(8,128)(2,1)S(1)} %get-tuple-element.83), channel_id=1, source_target_pairs={{0,16},{4,20},{8,24},{12,28},{16,0},{20,4},{24,8},{28,12},{1,17},{... | collective-permute-start | bytes 786440 | tf_op jit(solution)/shard_map/ppermute | solution.py:56
  262.5 40.3 %collective-permute-start.57 = (bf16[128,1024]{1,0:T(8,128)(2,1)S(1)}, bf16[128,1024]{1,0:T(8,128)(2,1)}, u32[]{:S(2)}, u32[]{:S(2)}) collective-permute-start(bf16[128,1024]{1,0:T(8,128)(2,1)S(1)} %get-tuple-element.82), channel_id=1, source_target_pairs={{0,24},{4,28},{8,0},{12,4},{16,8},{20,12},{24,16},{28,20},{1,25},{... | collective-permute-start | bytes 786440 | tf_op jit(solution)/shard_map/ppermute | solution.py:56
  317.6 35.4 %collective-permute-start.46 = (bf16[4,32,1024]{2,1,0:T(8,128)(2,1)}, bf16[4,32,1024]{2,1,0:T(8,128)(2,1)S(1)}, u32[]{:S(2)}, u32[]{:S(2)}) collective-permute-start(bf16[4,32,1024]{2,1,0:T(8,128)(2,1)} %fusion.45), channel_id=1, source_target_pairs={{0,4},{4,0},{8,12},{12,8},{16,20},{20,16},{24,28},{28,24},{1,5},{5... | collective-permute-start | bytes 786440 | tf_op jit(solution)/shard_map/ppermute | solution.py:56
  345.8 25.9 %collective-permute-start.42 = (bf16[4,128,768]{2,1,0:T(8,128)(2,1)S(1)}, bf16[4,128,768]{2,1,0:T(8,128)(2,1)S(1)}, u32[]{:S(2)}, u32[]{:S(2)}) collective-permute-start(bf16[4,128,768]{2,1,0:T(8,128)(2,1)S(1)} %fusion.33), channel_id=1, source_target_pairs={{0,4},{4,0},{8,12},{12,8},{16,20},{20,16},{24,28},{28,24},{1,5},{5... | collective-permute-start | bytes 2359304 | tf_op jit(solution)/shard_map/ppermute | solution.py:56
  353.1 31.6 %collective-permute-start.47 = (bf16[32,1024]{1,0:T(8,128)(2,1)S(1)}, bf16[32,1024]{1,0:T(8,128)(2,1)S(1)}, u32[]{:S(2)}, u32[]{:S(2)}) collective-permute-start(bf16[32,1024]{1,0:T(8,128)(2,1)S(1)} %get-tuple-element.99), channel_id=1, source_target_pairs={{0,8},{4,12},{8,16},{12,20},{16,24},{20,28},{24,0},{28,4},{1,9},{5... | collective-permute-start | bytes 196616 | tf_op jit(solution)/shard_map/ppermute | solution.py:56
  354.3 31.2 %collective-permute-start.48 = (bf16[32,1024]{1,0:T(8,128)(2,1)S(1)}, bf16[32,1024]{1,0:T(8,128)(2,1)S(1)}, u32[]{:S(2)}, u32[]{:S(2)}) collective-permute-start(bf16[32,1024]{1,0:T(8,128)(2,1)S(1)} %get-tuple-element.101), channel_id=1, source_target_pairs={{0,16},{4,20},{8,24},{12,28},{16,0},{20,4},{24,8},{28,12},{1,17},{... | collective-permute-start | bytes 196616 | tf_op jit(solution)/shard_map/ppermute | solution.py:56
  (79 other events, 713.1 us)

commit v3 on v2

--- a/solution.py
+++ b/solution.py
@@ -18,14 +18,6 @@
     centre = values - jnp.mean(values, axis=-1, keepdims=True)
     spread = jnp.mean(centre * centre, axis=-1, keepdims=True)
     return centre * lax.rsqrt(spread + eps)
-
-
-def gelu_tanh(values):
-    return (
-        0.5
-        * values
-        * (1.0 + jnp.tanh(0.7978845608028654 * (values + 0.044715 * values * values * values)))
-    )
 
 
 def contract_rows(left, right):
@@ -129,7 +121,7 @@
     x, core = place // 2, place % 2
     parts = parts.reshape((chips, 2, parts.shape[0] // groups) + parts.shape[1:])
     sent = pick(parts, 1 - core, 1).astype(jnp.bfloat16)
-    held = pick(parts, core, 1) + move_ctx(sent, 0, 1).astype(jnp.float32)
+    held = pick(parts, core, 1).astype(jnp.float32) + move_ctx(sent, 0, 1).astype(jnp.float32)
     summed = pick(held, x, 0)
     for step in range(1, chips):
         sent = pick(held, (x + step) % chips, 0).astype(jnp.bfloat16)
@@ -263,6 +255,88 @@
     )(qkv, grads, log_sums, seq_ids[None, :], seq_ids[:, None])
 
 
+def mlp_kernel(
+    in_ref,
+    grad_ref,
+    up_ref,
+    shift_ref,
+    down_ref,
+    act_ref,
+    pre_ref,
+    sums_ref,
+    out_ref,
+    back_ref,
+    out_acc,
+    back_acc,
+):
+    step = pl.program_id(0)
+    u = jnp.dot(in_ref[...], up_ref[...], preferred_element_type=jnp.float32) + shift_ref[...]
+    square = u * u
+    bent = jnp.tanh(0.7978845608028654 * (u * (1.0 + 0.044715 * square)))
+    half = 0.5 * (1.0 + bent)
+    act = (u * half).astype(jnp.bfloat16)
+    act_ref[...] = act
+    slope = half + 0.5 * u * (1.0 - bent * bent) * (
+        0.7978845608028654 * (1.0 + 0.134145 * square)
+    )
+    grad_pre = (contract_cols(grad_ref[...], down_ref[...]) * slope).astype(jnp.bfloat16)
+    pre_ref[...] = grad_pre
+    sums_ref[...] = jnp.sum(grad_pre.astype(jnp.float32), axis=0, keepdims=True)
+    out_part = jnp.dot(act, down_ref[...], preferred_element_type=jnp.float32)
+    back_part = contract_cols(grad_pre, up_ref[...])
+
+    @pl.when(step == 0)
+    def _():
+        out_acc[...] = out_part
+        back_acc[...] = back_part
+
+    @pl.when(step > 0)
+    def _():
+        out_acc[...] += out_part
+        back_acc[...] += back_part
+
+    @pl.when(step == pl.num_programs(0) - 1)
+    def _():
+        out_ref[...] = out_acc[...].astype(jnp.bfloat16)
+        back_ref[...] = back_acc[...].astype(jnp.bfloat16)
+
+
+def mlp(inputs, grads, up, shift, down):
+    rows, model = inputs.shape
+    hidden = up.shape[1]
+    block = min(256, hidden)
+    whole = pl.BlockSpec((rows, model), lambda i: (0, 0))
+    columns = pl.BlockSpec((rows, block), lambda i: (0, i))
+    line = pl.BlockSpec((1, block), lambda i: (0, i))
+    return pl.pallas_call(
+        mlp_kernel,
+        grid=(hidden // block,),
+        in_specs=[
+            whole,
+            whole,
+            pl.BlockSpec((model, block), lambda i: (0, i)),
+            line,
+            pl.BlockSpec((block, model), lambda i: (i, 0)),
+        ],
+        out_specs=(columns, columns, line, whole, whole),
+        out_shape=(
+            jax.ShapeDtypeStruct((rows, hidden), jnp.bfloat16),
+            jax.ShapeDtypeStruct((rows, hidden), jnp.bfloat16),
+            jax.ShapeDtypeStruct((1, hidden), jnp.float32),
+            jax.ShapeDtypeStruct((rows, model), jnp.bfloat16),
+            jax.ShapeDtypeStruct((rows, model), jnp.bfloat16),
+        ),
+        scratch_shapes=[pltpu.VMEM((rows, model), jnp.float32)] * 2,
+        compiler_params=pltpu.CompilerParams(vmem_limit_bytes=52 * 2**20),
+        cost_estimate=pl.CostEstimate(
+            flops=8 * rows * model * hidden,
+            bytes_accessed=8 * rows * model + 4 * rows * hidden + 4 * model * hidden,
+            transcendentals=rows * hidden,
+        ),
+        name="mlp",
+    )(inputs, grads, up, shift[None, :], down)
+
+
 def on_device(
     block_input,
     ln1_gain,
@@ -345,26 +419,22 @@
     norm_two = normalize(resid)
     h_two = (norm_two * gain_two + shift_two).astype(jnp.bfloat16)
     h_two_all = gather_rows(h_two)
-    up_proj = project(h_two_all, up_full)
-    pre_act = up_proj + up_here
-    act, gelu_back = jax.vjp(gelu_tanh, pre_act)
-    act_low = act.astype(jnp.bfloat16)
-    down_part = project(act_low, down_full)
-    output = (resid + reduce_rows(down_part) + down_shift).astype(jnp.bfloat16)
     live = (own_ids >= 0).astype(jnp.float32)
     grad_out = cotangent.astype(jnp.float32) * live[:, None]
     grad_low = grad_out.astype(jnp.bfloat16)
     down_shift_grad = jnp.sum(grad_low.astype(jnp.float32), axis=0)
     grad_all = jnp.where(group_ids[:, None] >= 0, cot_all, jnp.zeros_like(cot_all))
+    act_low, grad_pre, up_sums, down_part, back_part = mlp(
+        h_two_all, grad_all, up_full, up_here, down_full
+    )
+    grad_h_two = reduce_rows(back_part)
+    output = (resid + reduce_rows(down_part) + down_shift).astype(jnp.bfloat16)
     down_grad = weight_grad(act_low, grad_all)
-    grad_act = project_back(grad_all, down_full)
-    grad_pre = gelu_back(grad_act)[0].astype(jnp.bfloat16)
     up_grad = weight_grad(h_two_all, grad_pre)
-    up_sums = jnp.sum(grad_pre.astype(jnp.float32), axis=0)
+    up_sums = up_sums[0]
     up_shift_grad = lax.dynamic_update_slice_in_dim(
         jnp.zeros((FF,), jnp.float32), up_sums, place * hidden_here, 0
     )
-    grad_h_two = reduce_rows(project_back(grad_pre, up_full))
     gain_two_grad = jnp.sum(grad_h_two * norm_two, axis=0)
     shift_two_grad = jnp.sum(grad_h_two, axis=0)
     unused_two, norm_back_two = jax.vjp(normalize, resid)

time: 410 us -> 381 us (0.929)
  matrix products: 44.8 us -> 21.4 us
  local copies, waits for them, and re-layouts: 89.7 us -> 68 us
  Pallas kernels: 20.9 us -> 41.2 us
  waiting for transfers between devices: 154 us -> 140 us
  starting transfers between devices: 55 us -> 68 us
    ppermute x36, waiting for transfers between devices: 120 us -> 97.4 us  [move_fsdp(): return lax.ppermute(values, 'fsdp', pairs)]
    pallas_call x0 -> x1, Pallas kernels: none -> 20 us  [mlp(): pl.pallas_call(mlp_kernel, grid=(hidden // block,), in_specs=[whole, whol...]
    dot_general x4 -> x2, matrix products: 20.8 us -> 6.04 us  [contract_cols(): lax.dot_general(left, right, (((1,), (1,)), ((), ())), preferred_element_...]
    dot_general x4 -> x2, matrix products: 15.1 us -> 2.51 us  [project(): return jnp.dot(inputs, weight, preferred_element_type=jnp.float32)]
    ppermute x22, waiting for transfers between devices: 33.8 us -> 42.5 us  [move_ctx(): return lax.ppermute(values, 'ctx', pairs)]
    dot_general x2 -> x0, local copies, waits for them, and re-layouts: 8.29 us -> none  [the longest x1 4.32 us: contract_cols(): lax.dot_general(left, right, (((1,), (1,)), ((), ())), preferred_element_...]
    ppermute x36, starting transfers between devices: 46.2 us -> 53.7 us  [move_fsdp(): return lax.ppermute(values, 'fsdp', pairs)]
    ppermute x22, starting transfers between devices: 8.78 us -> 14.2 us  [move_ctx(): return lax.ppermute(values, 'ctx', pairs)]
  transfers between devices with their start and end apart: 58 -> 58, of which waited for: 23 -> 27; matrix products, arithmetic and copies ran while one was open for 33% -> 27% of each run, Pallas kernels for 5% -> 6%
where the time goes in v3:
time: 381 us; the launch traced here: 376 us
  waiting for transfers between devices  140 us (37%)
  local copies, waits for them, and re-layouts  68 us (18%)
  starting transfers between devices  68 us (18%)
  Pallas kernels  41.2 us (11%)
  other arithmetic  35.6 us (9%)
  matrix products  21.4 us (6%)
    ppermute x36, waiting for transfers between devices, move_fsdp(): return lax.ppermute(values, 'fsdp', pairs)  97.4 us
    ppermute x36, starting transfers between devices, move_fsdp(): return lax.ppermute(values, 'fsdp', pairs)  53.7 us
    ppermute x22, waiting for transfers between devices, move_ctx(): return lax.ppermute(values, 'ctx', pairs)  42.5 us
    pallas_call x1, Pallas kernels, mlp(): pl.pallas_call(mlp_kernel, grid=(hidden // block,), in_specs=[whole, whol...  20 us
    unnamed x103, local copies, waits for them, and re-layouts  17.7 us
    dynamic_update_slice x31, local copies, waits for them, and re-layouts, put(): return lax.dynamic_update_index_in_dim(buffer, values, place, axis)  17.6 us
    ppermute x22, starting transfers between devices, move_ctx(): return lax.ppermute(values, 'ctx', pairs)  14.2 us
    dot_general x4, matrix products, contract_rows(): lax.dot_general(left, right, (((0,), (0,)), ((), ())), preferred_element_...  12.9 us
  transfers between devices with their start and end apart: 58, of which 27 were waited for; matrix products, arithmetic and copies ran while one was open for 27% of the time, Pallas kernels for 6%

profile of v3, /device:TPU:8, one launch (start us, length us, event | category | flops | bytes accessed | tf_op | source)
XLA Modules:
  0.0 376.1 jit_solution(5983757197067828154)
XLA Ops:
  28.5 15.1 %collective-permute-done.9 = bf16[32,1024]{1,0:T(8,128)(2,1)S(1)} collective-permute-done((bf16[32,1024]{1,0:T(8,128)(2,1)}, bf16[32,1024]{1,0:T(8,128)(2,1)S(1)}, u32[]{:S(2)}, u32[]{:S(2)}) %collective-permute-start.9) | collective-permute-done | bytes 65568 | tf_op jit(solution)/shard_map/ppermute | solution.py:48
  45.8 9.6 %collective-permute-start.19 = (bf16[128,1024]{1,0:T(8,128)(2,1)}, bf16[128,1024]{1,0:T(8,128)(2,1)}, u32[]{:S(2)}, u32[]{:S(2)}) collective-permute-start(bf16[128,1024]{1,0:T(8,128)(2,1)} %param.24), channel_id=1, source_target_pairs={{0,8},{4,12},{8,16},{12,20},{16,24},{20,28},{24,0},{28,4},{1,9},{5... | collective-permute-start | bytes 786440 | tf_op jit(solution)/shard_map/ppermute | solution.py:48
  55.5 14.0 %collective-permute-done.5 = bf16[144,768]{0,1:T(8,128)(2,1)} collective-permute-done((bf16[144,768]{0,1:T(8,128)(2,1)}, bf16[144,768]{0,1:T(8,128)(2,1)}, u32[]{:S(2)}, u32[]{:S(2)}) %collective-permute-start.5) | collective-permute-done | bytes 221216 | tf_op jit(solution)/shard_map/ppermute | solution.py:48
  75.4 5.4 %collective-permute-done.25 = bf16[128,1024]{1,0:T(8,128)(2,1)} collective-permute-done((bf16[128,1024]{1,0:T(8,128)(2,1)}, bf16[128,1024]{1,0:T(8,128)(2,1)}, u32[]{:S(2)}, u32[]{:S(2)}) %collective-permute-start.25) | collective-permute-done | bytes 262176 | tf_op jit(solution)/shard_map/ppermute | solution.py:48
  93.2 3.8 %collective-permute-done.10 = bf16[4,32,1024]{2,1,0:T(8,128)(2,1)S(1)} collective-permute-done((bf16[4,32,1024]{2,1,0:T(8,128)(2,1)S(1)}, bf16[4,32,1024]{2,1,0:T(8,128)(2,1)S(1)}, u32[]{:S(2)}, u32[]{:S(2)}) %collective-permute-start.10) | collective-permute-done | bytes 262176 | tf_op jit(solution)/shard_map/ppermute | solution.py:48
  101.0 3.6 collective-permute-done.17
  110.5 9.1 %collective-permute-done.6 = bf16[4,144,768]{2,1,0:T(8,128)(2,1)S(1)} collective-permute-done((bf16[4,144,768]{2,1,0:T(8,128)(2,1)S(1)}, bf16[4,144,768]{2,1,0:T(8,128)(2,1)S(1)}, u32[]{:S(2)}, u32[]{:S(2)}) %collective-permute-start.6) | collective-permute-done | bytes 884768 | tf_op jit(solution)/shard_map/ppermute | solution.py:48
  124.8 9.8 %attend.1 = (bf16[1024,256]{1,0:T(8,128)(2,1)S(1)}, f32[4,1024]{1,0:T(4,128)S(1)}) custom-call(bf16[1024,768]{1,0:T(8,128)(2,1)S(1)} %add_convert_fusion.2.qkv_ref, s32[1,1024]{1,0:T(1,128)S(1)} %copy-done, s32[1024,1]{1,0:T(8,128)S(1)} %copy.66.ids_col_ref), custom_call_target="tpu_custom_call" | custom-call | flops 4294967296 | bytes 2097152 | tf_op jit(solution)/shard_map/attend/pallas_call | solution.py:225
  146.5 9.7 %collective-permute-done.12 = bf16[256,1024]{1,0:T(8,128)(2,1)S(1)} collective-permute-done((bf16[256,1024]{1,0:T(8,128)(2,1)S(1)}, bf16[256,1024]{1,0:T(8,128)(2,1)S(1)}, u32[]{:S(2)}, u32[]{:S(2)}) %collective-permute-start.12) | collective-permute-done | bytes 524320 | tf_op jit(solution)/shard_map/ppermute | solution.py:58
  164.2 6.8 %collective-permute-done.14 = bf16[256,1024]{1,0:T(8,128)(2,1)S(1)} collective-permute-done((bf16[256,1024]{1,0:T(8,128)(2,1)S(1)}, bf16[256,1024]{1,0:T(8,128)(2,1)S(1)}, u32[]{:S(2)}, u32[]{:S(2)}) %collective-permute-start.14) | collective-permute-done | bytes 524320 | tf_op jit(solution)/shard_map/ppermute | solution.py:58
  174.4 20.0 %mlp.1 = (bf16[1024,1024]{1,0:T(8,128)(2,1)}, bf16[1024,1024]{1,0:T(8,128)(2,1)}, f32[1,1024]{1,0:T(1,128)S(1)}, bf16[1024,1024]{1,0:T(8,128)(2,1)}, bf16[1024,1024]{1,0:T(8,128)(2,1)}) custom-call(bf16[1024,1024]{1,0:T(8,128)(2,1)} %bitcast.399, bf16[1024,1024]{1,0:T(8,128)(2,1)} %bitcast_select_fusion.grad_ref, bf16[1024,1024]{1,0:T(8,128)(2,1)} %bitcast.415, ...), custom_call_target="tpu_custom_call" | custom-call | flops 8589934592 | bytes 16777216 | tf_op jit(solution)/shard_map/mlp/pallas_call | solution.py:311
  194.3 3.9 %copy.87 = bf16[1024,1024]{1,0:T(8,128)(2,1)} copy(bf16[1024,1024]{0,1:T(8,128)(2,1)} %bitcast.417) | data formatting | bytes 4194304 | tf_op jit(solution)/shard_map/dot_general | solution.py:24
  198.3 4.5 %fusion.79 = f32[4,2,128,1024]{3,2,1,0:T(8,128)S(1)} fusion(bf16[4,2,128,1024]{3,2,1,0:T(8,128)(2,1)} %bitcast.420, bf16[1024,1024,1,1]{1,0,3,2:T(8,128)(2,1)} %bitcast.409), kind=kOutput, calls=%fused_computation.241 | convolution fusion | flops 2147483648 | bytes 8388608 | tf_op jit(solution)/shard_map/dot_general | solution.py:24
  208.5 3.9 %copy.86 = bf16[1024,1024]{1,0:T(8,128)(2,1)} copy(bf16[1024,1024]{0,1:T(8,128)(2,1)} %bitcast.400) | data formatting | bytes 4194304 | tf_op jit(solution)/shard_map/dot_general | solution.py:24
  215.0 4.1 %fusion.1 = f32[4,2,128,1024]{3,2,1,0:T(8,128)S(1)} fusion(bf16[4,2,128,1024]{3,2,1,0:T(8,128)(2,1)S(1)} %bitcast.416, bf16[1024,1024]{1,0:T(8,128)(2,1)} %get-tuple-element.26), kind=kOutput, calls=%fused_computation.12 | convolution fusion | flops 2147483648 | bytes 8388608 | tf_op jit(solution)/shard_map/dot_general | solution.py:24
  219.8 12.4 %collective-permute-done.54 = bf16[4,128,1024]{2,1,0:T(8,128)(2,1)} collective-permute-done((bf16[4,128,1024]{2,1,0:T(8,128)(2,1)}, bf16[4,128,1024]{2,1,0:T(8,128)(2,1)}, u32[]{:S(2)}, u32[]{:S(2)}) %collective-permute-start.54) | collective-permute-done | bytes 1048608 | tf_op jit(solution)/shard_map/ppermute | solution.py:48
  241.9 12.2 %collective-permute-done.50 = bf16[4,128,1024]{2,1,0:T(8,128)(2,1)S(1)} collective-permute-done((bf16[4,128,1024]{2,1,0:T(8,128)(2,1)S(1)}, bf16[4,128,1024]{2,1,0:T(8,128)(2,1)S(1)}, u32[]{:S(2)}, u32[]{:S(2)}) %collective-permute-start.50) | collective-permute-done | bytes 1048608 | tf_op jit(solution)/shard_map/ppermute | solution.py:48
  257.5 10.1 %collective-permute-done.28 = bf16[256,1024]{1,0:T(8,128)(2,1)S(1)} collective-permute-done((bf16[256,1024]{1,0:T(8,128)(2,1)S(1)}, bf16[256,1024]{1,0:T(8,128)(2,1)S(1)}, u32[]{:S(2)}, u32[]{:S(2)}) %collective-permute-start.28) | collective-permute-done | bytes 524320 | tf_op jit(solution)/shard_map/ppermute | solution.py:58
  293.6 11.4 %attend_back.1 = bf16[1024,768]{1,0:T(8,128)(2,1)S(1)} custom-call(bf16[1024,768]{1,0:T(8,128)(2,1)S(1)} %copy-done.2, bf16[1024,256]{1,0:T(8,128)(2,1)S(1)} %convolution_convert_fusion.grad_ref, f32[4,1024]{1,0:T(4,128)S(1)} %get-tuple-element.24.lse_ref, s32[1,1024]{1,0:T(1,128)S(1)} %copy-done, s32[1024,1]{1,0:T(8,128)S(1)} %copy.66.ids_col_ref), custom_call_target="tpu_custom_call" | custom-call | flops 10737418240 | bytes 3670016 | tf_op jit(solution)/shard_map/attend_back/pallas_call | solution.py:244
  305.4 5.3 %fusion.68 = (f32[1024]{0:T(1024)S(1)}, f32[1024]{0:T(1024)S(1)}, bf16[1024,1024]{1,0:T(8,128)(2,1)}, f32[1024,1024]{1,0:T(8,128)}) fusion(f32[1024]{0:T(1024)S(1)} %bitcast.436, f32[1024]{0:T(1024)S(1)} %bitcast.437, bf16[4,256,1024]{2,1,0:T(8,128)(2,1)} %bitcast_dynamic-update-slice_fusion.12, f32[1024]{0:T(1024)S(1)} %get-tuple-element.120, ...), kind=kOutput, calls=%fused_computation.232 | convolution fusion | flops 1620047872 | bytes 11558912 | tf_op jit(solution)/shard_map/dot_general | solution.py:30
  310.7 4.0 %copy.85 = bf16[1024,1024]{1,0:T(8,128)(2,1)} copy(bf16[1024,1024]{0,1:T(8,128)(2,1)} %bitcast.418) | data formatting | bytes 4194304 | tf_op jit(solution)/shard_map/dot_general | solution.py:24
  314.6 3.5 fusion.3
  330.3 8.9 %collective-permute-done.35 = bf16[256,1024]{1,0:T(8,128)(2,1)S(1)} collective-permute-done((bf16[256,1024]{1,0:T(8,128)(2,1)S(1)}, bf16[256,1024]{1,0:T(8,128)(2,1)S(1)}, u32[]{:S(2)}, u32[]{:S(2)}) %collective-permute-start.35) | collective-permute-done | bytes 524320 | tf_op jit(solution)/shard_map/ppermute | solution.py:58
  358.7 4.3 %collective-permute-done.49 = bf16[32,1024]{1,0:T(8,128)(2,1)S(1)} collective-permute-done((bf16[32,1024]{1,0:T(8,128)(2,1)S(1)}, bf16[32,1024]{1,0:T(8,128)(2,1)S(1)}, u32[]{:S(2)}, u32[]{:S(2)}) %collective-permute-start.49) | collective-permute-done | bytes 65568 | tf_op jit(solution)/shard_map/ppermute | solution.py:48
  (353 shorter events, 178.5 us)
Async XLA Ops:
  0.7 70.0 %collective-permute-start.23 = (bf16[128,1024]{1,0:T(8,128)(2,1)}, bf16[128,1024]{1,0:T(8,128)(2,1)}, u32[]{:S(2)}, u32[]{:S(2)}) collective-permute-start(bf16[128,1024]{1,0:T(8,128)(2,1)} %param.26), channel_id=1, source_target_pairs={{0,8},{4,12},{8,16},{12,20},{16,24},{20,28},{24,0},{28,4},{1,9},{5... | collective-permute-start | bytes 786440 | tf_op jit(solution)/shard_map/ppermute | solution.py:48
  2.4 71.3 %collective-permute-start.24 = (bf16[128,1024]{1,0:T(8,128)(2,1)}, bf16[128,1024]{1,0:T(8,128)(2,1)}, u32[]{:S(2)}, u32[]{:S(2)}) collective-permute-start(bf16[128,1024]{1,0:T(8,128)(2,1)} %param.26), channel_id=1, source_target_pairs={{0,16},{4,20},{8,24},{12,28},{16,0},{20,4},{24,8},{28,12},{1,17},{... | collective-permute-start | bytes 786440 | tf_op jit(solution)/shard_map/ppermute | solution.py:48
  4.3 22.5 %collective-permute-start.8 = (bf16[32,1024]{1,0:T(8,128)(2,1)}, bf16[32,1024]{1,0:T(8,128)(2,1)S(1)}, u32[]{:S(2)}, u32[]{:S(2)}) collective-permute-start(bf16[32,1024]{1,0:T(8,128)(2,1)} %param.20), channel_id=1, source_target_pairs={{0,16},{4,20},{8,24},{12,28},{16,0},{20,4},{24,8},{28,12},{1,17},{... | collective-permute-start | bytes 196616 | tf_op jit(solution)/shard_map/ppermute | solution.py:48
  7.8 35.8 %collective-permute-start.9 = (bf16[32,1024]{1,0:T(8,128)(2,1)}, bf16[32,1024]{1,0:T(8,128)(2,1)S(1)}, u32[]{:S(2)}, u32[]{:S(2)}) collective-permute-start(bf16[32,1024]{1,0:T(8,128)(2,1)} %param.20), channel_id=1, source_target_pairs={{0,24},{4,28},{8,0},{12,4},{16,8},{20,12},{24,16},{28,20},{1,25},{... | collective-permute-start | bytes 196616 | tf_op jit(solution)/shard_map/ppermute | solution.py:48
  43.6 25.9 %collective-permute-start.5 = (bf16[144,768]{0,1:T(8,128)(2,1)}, bf16[144,768]{0,1:T(8,128)(2,1)}, u32[]{:S(2)}, u32[]{:S(2)}) collective-permute-start(bf16[144,768]{0,1:T(8,128)(2,1)} %get-tuple-element.112), channel_id=1, source_target_pairs={{0,24},{4,28},{8,0},{12,4},{16,8},{20,12},{24,16},{28,20},{1,25},{... | collective-permute-start | bytes 663560 | tf_op jit(solution)/shard_map/ppermute | solution.py:48
  43.9 36.9 %collective-permute-start.25 = (bf16[128,1024]{1,0:T(8,128)(2,1)}, bf16[128,1024]{1,0:T(8,128)(2,1)}, u32[]{:S(2)}, u32[]{:S(2)}) collective-permute-start(bf16[128,1024]{1,0:T(8,128)(2,1)} %param.26), channel_id=1, source_target_pairs={{0,24},{4,28},{8,0},{12,4},{16,8},{20,12},{24,16},{28,20},{1,25},{... | collective-permute-start | bytes 786440 | tf_op jit(solution)/shard_map/ppermute | solution.py:48
  45.8 38.2 %collective-permute-start.19 = (bf16[128,1024]{1,0:T(8,128)(2,1)}, bf16[128,1024]{1,0:T(8,128)(2,1)}, u32[]{:S(2)}, u32[]{:S(2)}) collective-permute-start(bf16[128,1024]{1,0:T(8,128)(2,1)} %param.24), channel_id=1, source_target_pairs={{0,8},{4,12},{8,16},{12,20},{16,24},{20,28},{24,0},{28,4},{1,9},{5... | collective-permute-start | bytes 786440 | tf_op jit(solution)/shard_map/ppermute | solution.py:48
  73.7 25.1 %collective-permute-start = (bf16[256,1024]{1,0:T(8,128)(2,1)S(1)}, bf16[256,1024]{1,0:T(8,128)(2,1)S(1)}, u32[]{:S(2)}, u32[]{:S(2)}) collective-permute-start(bf16[256,1024]{1,0:T(8,128)(2,1)S(1)} %copy-done.6), channel_id=1, source_target_pairs={{0,1},{1,0},{2,3},{3,2},{4,5},{5,4},{6,7},{7,6},{8,9},{9,8},{10,11... | collective-permute-start | bytes 1572872 | tf_op jit(solution)/shard_map/ppermute | solution.py:58
  83.9 51.7 %collective-permute-start.16 = (bf16[256,1024]{1,0:T(8,128)(2,1)S(1)}, bf16[256,1024]{1,0:T(8,128)(2,1)S(1)}, u32[]{:S(2)}, u32[]{:S(2)}) collective-permute-start(bf16[256,1024]{1,0:T(8,128)(2,1)S(1)} %copy-done.9), channel_id=1, source_target_pairs={{0,1},{1,0},{2,3},{3,2},{4,5},{5,4},{6,7},{7,6},{8,9},{9,8},{10,11... | collective-permute-start | bytes 1572872 | tf_op jit(solution)/shard_map/ppermute | solution.py:58
  97.0 22.6 %collective-permute-start.6 = (bf16[4,144,768]{2,1,0:T(8,128)(2,1)S(1)}, bf16[4,144,768]{2,1,0:T(8,128)(2,1)S(1)}, u32[]{:S(2)}, u32[]{:S(2)}) collective-permute-start(bf16[4,144,768]{2,1,0:T(8,128)(2,1)S(1)} %constant_dynamic-update-slice_fusion.1), channel_id=1, source_target_pairs={{0,4},{4,0},{8,12},{12,8},{16,20},{20,16},{24,28},{28,24},{1,5},{5... | collective-permute-start | bytes 2654216 | tf_op jit(solution)/shard_map/ppermute | solution.py:48
  98.8 60.1 %collective-permute-start.26 = (bf16[4,128,1024]{2,1,0:T(8,128)(2,1)}, bf16[4,128,1024]{2,1,0:T(8,128)(2,1)S(1)}, u32[]{:S(2)}, u32[]{:S(2)}) collective-permute-start(bf16[4,128,1024]{2,1,0:T(8,128)(2,1)} %bitcast_dynamic-update-slice_fusion.16), channel_id=1, source_target_pairs={{0,4},{4,0},{8,12},{12,8},{16,20},{20,16},{24,28},{28,24},{1,5},{5... | collective-permute-start | bytes 3145736 | tf_op jit(solution)/shard_map/ppermute | solution.py:48
  104.6 58.1 %collective-permute-start.22 = (bf16[4,128,1024]{2,1,0:T(8,128)(2,1)}, bf16[4,128,1024]{2,1,0:T(8,128)(2,1)S(1)}, u32[]{:S(2)}, u32[]{:S(2)}) collective-permute-start(bf16[4,128,1024]{2,1,0:T(8,128)(2,1)} %bitcast_dynamic-update-slice_fusion.20), channel_id=1, source_target_pairs={{0,4},{4,0},{8,12},{12,8},{16,20},{20,16},{24,28},{28,24},{1,5},{5... | collective-permute-start | bytes 3145736 | tf_op jit(solution)/shard_map/ppermute | solution.py:48
  105.4 32.0 %collective-permute-start.18 = (bf16[256,1024]{1,0:T(8,128)(2,1)S(1)}, bf16[256,1024]{1,0:T(8,128)(2,1)S(1)}, u32[]{:S(2)}, u32[]{:S(2)}) collective-permute-start(bf16[256,1024]{1,0:T(8,128)(2,1)S(1)} %collective-permute-done.17), channel_id=1, source_target_pairs={{0,1},{1,0},{2,3},{3,2},{4,5},{5,4},{6,7},{7,6},{8,9},{9,8},{10,11... | collective-permute-start | bytes 1572872 | tf_op jit(solution)/shard_map/ppermute | solution.py:58
  205.9 26.3 %collective-permute-start.54 = (bf16[4,128,1024]{2,1,0:T(8,128)(2,1)}, bf16[4,128,1024]{2,1,0:T(8,128)(2,1)}, u32[]{:S(2)}, u32[]{:S(2)}) collective-permute-start(bf16[4,128,1024]{2,1,0:T(8,128)(2,1)} %fusion.13), channel_id=1, source_target_pairs={{0,4},{4,0},{8,12},{12,8},{16,20},{20,16},{24,28},{28,24},{1,5},{5... | collective-permute-start | bytes 3145736 | tf_op jit(solution)/shard_map/ppermute | solution.py:48
  213.9 26.0 %collective-permute-start.27 = (bf16[2,256,1024]{2,1,0:T(8,128)(2,1)S(1)}, bf16[2,256,1024]{2,1,0:T(8,128)(2,1)S(1)}, u32[]{:S(2)}, u32[]{:S(2)}) collective-permute-start(bf16[2,256,1024]{2,1,0:T(8,128)(2,1)S(1)} %dynamic-slice_bitcast_fusion.1), channel_id=1, source_target_pairs={{0,1},{1,0},{2,3},{3,2},{4,5},{5,4},{6,7},{7,6},{8,9},{9,8},{10,11... | collective-permute-start | bytes 3145736 | tf_op jit(solution)/shard_map/ppermute | solution.py:58
  214.4 23.0 %collective-permute-start.29 = (bf16[2,256,1024]{2,1,0:T(8,128)(2,1)S(1)}, bf16[2,256,1024]{2,1,0:T(8,128)(2,1)S(1)}, u32[]{:S(2)}, u32[]{:S(2)}) collective-permute-start(bf16[2,256,1024]{2,1,0:T(8,128)(2,1)S(1)} %dynamic-slice_bitcast_fusion), channel_id=1, source_target_pairs={{0,1},{1,0},{2,3},{3,2},{4,5},{5,4},{6,7},{7,6},{8,9},{9,8},{10,11... | collective-permute-start | bytes 3145736 | tf_op jit(solution)/shard_map/ppermute | solution.py:58
  219.2 34.9 %collective-permute-start.50 = (bf16[4,128,1024]{2,1,0:T(8,128)(2,1)S(1)}, bf16[4,128,1024]{2,1,0:T(8,128)(2,1)S(1)}, u32[]{:S(2)}, u32[]{:S(2)}) collective-permute-start(bf16[4,128,1024]{2,1,0:T(8,128)(2,1)S(1)} %fusion.12), channel_id=1, source_target_pairs={{0,4},{4,0},{8,12},{12,8},{16,20},{20,16},{24,28},{28,24},{1,5},{5... | collective-permute-start | bytes 3145736 | tf_op jit(solution)/shard_map/ppermute | solution.py:48
  234.0 39.4 %collective-permute-start.55 = (bf16[128,1024]{1,0:T(8,128)(2,1)S(1)}, bf16[128,1024]{1,0:T(8,128)(2,1)S(1)}, u32[]{:S(2)}, u32[]{:S(2)}) collective-permute-start(bf16[128,1024]{1,0:T(8,128)(2,1)S(1)} %get-tuple-element.88), channel_id=1, source_target_pairs={{0,8},{4,12},{8,16},{12,20},{16,24},{20,28},{24,0},{28,4},{1,9},{5... | collective-permute-start | bytes 786440 | tf_op jit(solution)/shard_map/ppermute | solution.py:48
  234.1 39.4 %collective-permute-start.56 = (bf16[128,1024]{1,0:T(8,128)(2,1)S(1)}, bf16[128,1024]{1,0:T(8,128)(2,1)S(1)}, u32[]{:S(2)}, u32[]{:S(2)}) collective-permute-start(bf16[128,1024]{1,0:T(8,128)(2,1)S(1)} %get-tuple-element.90), channel_id=1, source_target_pairs={{0,16},{4,20},{8,24},{12,28},{16,0},{20,4},{24,8},{28,12},{1,17},{... | collective-permute-start | bytes 786440 | tf_op jit(solution)/shard_map/ppermute | solution.py:48
  237.4 39.2 %collective-permute-start.57 = (bf16[128,1024]{1,0:T(8,128)(2,1)S(1)}, bf16[128,1024]{1,0:T(8,128)(2,1)}, u32[]{:S(2)}, u32[]{:S(2)}) collective-permute-start(bf16[128,1024]{1,0:T(8,128)(2,1)S(1)} %get-tuple-element.89), channel_id=1, source_target_pairs={{0,24},{4,28},{8,0},{12,4},{16,8},{20,12},{24,16},{28,20},{1,25},{... | collective-permute-start | bytes 786440 | tf_op jit(solution)/shard_map/ppermute | solution.py:48
  290.7 36.3 %collective-permute-start.46 = (bf16[4,32,1024]{2,1,0:T(8,128)(2,1)}, bf16[4,32,1024]{2,1,0:T(8,128)(2,1)S(1)}, u32[]{:S(2)}, u32[]{:S(2)}) collective-permute-start(bf16[4,32,1024]{2,1,0:T(8,128)(2,1)} %fusion.32), channel_id=1, source_target_pairs={{0,4},{4,0},{8,12},{12,8},{16,20},{20,16},{24,28},{28,24},{1,5},{5... | collective-permute-start | bytes 786440 | tf_op jit(solution)/shard_map/ppermute | solution.py:48
  319.9 26.0 %collective-permute-start.42 = (bf16[4,128,768]{2,1,0:T(8,128)(2,1)S(1)}, bf16[4,128,768]{2,1,0:T(8,128)(2,1)S(1)}, u32[]{:S(2)}, u32[]{:S(2)}) collective-permute-start(bf16[4,128,768]{2,1,0:T(8,128)(2,1)S(1)} %fusion.20), channel_id=1, source_target_pairs={{0,4},{4,0},{8,12},{12,8},{16,20},{20,16},{24,28},{28,24},{1,5},{5... | collective-permute-start | bytes 2359304 | tf_op jit(solution)/shard_map/ppermute | solution.py:48
  327.1 31.0 %collective-permute-start.47 = (bf16[32,1024]{1,0:T(8,128)(2,1)S(1)}, bf16[32,1024]{1,0:T(8,128)(2,1)S(1)}, u32[]{:S(2)}, u32[]{:S(2)}) collective-permute-start(bf16[32,1024]{1,0:T(8,128)(2,1)S(1)} %get-tuple-element.106), channel_id=1, source_target_pairs={{0,8},{4,12},{8,16},{12,20},{16,24},{20,28},{24,0},{28,4},{1,9},{5... | collective-permute-start | bytes 196616 | tf_op jit(solution)/shard_map/ppermute | solution.py:48
  328.3 30.5 %collective-permute-start.48 = (bf16[32,1024]{1,0:T(8,128)(2,1)S(1)}, bf16[32,1024]{1,0:T(8,128)(2,1)S(1)}, u32[]{:S(2)}, u32[]{:S(2)}) collective-permute-start(bf16[32,1024]{1,0:T(8,128)(2,1)S(1)} %get-tuple-element.108), channel_id=1, source_target_pairs={{0,16},{4,20},{8,24},{12,28},{16,0},{20,4},{24,8},{28,12},{1,17},{... | collective-permute-start | bytes 196616 | tf_op jit(solution)/shard_map/ppermute | solution.py:48
  (74 other events, 684.9 us)
